TPU v7x, 256 devices: a whole 4x4x8 slice. The times are simulated.
256 devices in a mesh: section: 8 (over y, core), dp: 32 (over x, z).
Axes of the slice: x: 4, y: 4, z: 8, core: 2. Of those that a mesh axis runs over, the one named last changes fastest.
Arguments:
- tokens: bfloat16 [4, 1024, 2048], P(None, 'dp'), may hold values from -6 to 6
- norm_gain: bfloat16 [8, 2048], P('section'), may hold values from 0.25 to 1.75
- router_weight: bfloat16 [8, 2048, 32], P('section'), may hold values from -0.125 to 0.125
- gate_weight: bfloat16 [8, 32, 2048, 768], P('section', 'dp'), may hold values from -0.125 to 0.125
- up_weight: bfloat16 [8, 32, 2048, 768], P('section', 'dp'), may hold values from -0.125 to 0.125
- down_weight: bfloat16 [8, 32, 768, 2048], P('section', 'dp'), may hold values from -0.21875 to 0.21875
- routing: int32 [8, 4, 1024, 6], P('section', None, 'dp'), may hold values from 0 to 31, all different within a row; in each aligned block of 32 rows (0 to 31, 32 to 63, ..., all dimensions but the last counted through in order) at most 7 rows name the same one
Outputs:
- layer_outputs: bfloat16 [8, 4, 1024, 2048], P('section', None, 'dp')
- router_grad: float32 [8, 2048, 32], P('section', 'dp')
Inputs may be any that keep to these rules, and one draw needn't show every extreme that they name: `routing`: each token names 6 different experts. Among one index of dp's 32 tokens of one micro-batch and layer, at most 7 name the same expert, and in some of these blocks exactly 7 do.
All inputs are finite; a program needn't handle non-finite values.
Results may differ from a plain program's by a relative error of at most 0.019.
Values may be sent and summed in bfloat16 or wider, within the bound.
A program may use at most 64 MiB of HBM per device.

v0:
```python
import jax
import jax.numpy as jnp
from jax import lax
from jax.sharding import Mesh
from jax.sharding import PartitionSpec as P

DP = ("dp_0", "dp_1")


EPSILON = 1e-06


def over_axes(shard, axes):
    for axis in axes:
        shard = lax.psum(shard, axis)
    return shard


def from_behind(value, axis, steps):
    count = lax.axis_size(axis)
    initial, last = (max(0, -steps), min(count, count - steps))
    return lax.ppermute(value, axis, [(source, source + steps) for source in range(initial, last)])


def cut_along(shard, dim, peers):
    shape = shard.shape
    pieces = shard.reshape(*shape[:dim], peers, shape[dim] // peers, *shape[dim + 1 :])
    return jnp.moveaxis(pieces, dim, 0)


def summed_on_arrival(shard, axis, dim):
    pieces = cut_along(shard, dim, lax.axis_size(axis))
    arrived = lax.all_to_all(pieces, axis, split_axis=0, concat_axis=0, tiled=True)
    return arrived.astype(jnp.float32).sum(axis=0)


def normalize(states, gain):
    values = states.astype(jnp.float32)
    mean_square = jnp.mean(values * values, axis=-1, keepdims=True)
    return (values * lax.rsqrt(mean_square + EPSILON) * gain.astype(jnp.float32)).astype(
        jnp.bfloat16
    )


def expert_ffn(rows, w_gate, w_up, w_down):
    gated = jnp.dot(rows, w_gate, preferred_element_type=jnp.float32)
    upward = jnp.dot(rows, w_up, preferred_element_type=jnp.float32)
    hidden = (jax.nn.silu(gated) * upward).astype(jnp.bfloat16)
    return jnp.dot(hidden, w_down, preferred_element_type=jnp.float32).astype(jnp.bfloat16)


def slope_of(probs, share):
    return probs * (share - jnp.sum(probs * share, axis=-1, keepdims=True))


def outer_rows(normed_rows, slope_rows):
    return lax.dot_general(
        normed_rows.astype(jnp.float32),
        slope_rows,
        (((0,), (0,)), ((), ())),
        precision=lax.Precision.HIGHEST,
    )


def place(stack, index, value, active):
    previous = lax.dynamic_index_in_dim(stack, index, 0, keepdims=False)
    return lax.dynamic_update_index_in_dim(stack, jnp.where(active, value, previous), index, 0)


def on_device(tokens, norm_gain, router_weight, gate_weight, up_weight, down_weight, routing):
    sections = lax.axis_size("section")
    replicas = lax.axis_size(DP)
    position = lax.axis_index("section")
    micro = tokens.shape[0]
    rows = tokens.shape[1]
    width = tokens.shape[2]
    experts = router_weight.shape[2]
    chosen_count = routing.shape[3]
    slots = min(rows, rows * chosen_count // experts + 1)
    total_rows = micro * rows * replicas
    gain = norm_gain[0]
    w_router = router_weight[0]
    w_gate = gate_weight[0, 0]
    w_up = up_weight[0, 0]
    w_down = down_weight[0, 0]
    expert_ids = jnp.arange(experts, dtype=jnp.int32)
    hot_all = (routing[0][..., None] == expert_ids).astype(jnp.int32).sum(axis=2)
    local_counts = jnp.sum(hot_all, axis=(0, 1))
    slot_ids = jnp.arange(slots, dtype=jnp.int32)

    def section_work(states, hot, active):
        normed = normalize(states, gain)
        logits = jnp.dot(normed, w_router, preferred_element_type=jnp.float32)
        exps = jnp.exp(logits)
        probs = exps / jnp.sum(exps, axis=-1, keepdims=True)
        rank = jnp.cumsum(hot, axis=0) - hot
        match = ((hot.T[:, None, :] == 1) & (rank.T[:, None, :] == slot_ids[None, :, None])).astype(
            jnp.bfloat16
        )
        sent = jnp.einsum("ect,td->ecd", match, normed, preferred_element_type=jnp.float32).astype(
            jnp.bfloat16
        )

        def compute(flat):
            return expert_ffn(flat, w_gate, w_up, w_down)

        def skipped(flat):
            return jnp.zeros((flat.shape[0], width), jnp.bfloat16)

        received = lax.all_to_all(sent, DP, split_axis=0, concat_axis=0, tiled=True)
        flat = received.reshape(-1, width)
        produced = lax.cond(active, compute, skipped, flat)
        returned = lax.all_to_all(
            produced.reshape(received.shape), DP, split_axis=0, concat_axis=0, tiled=True
        )
        chosen = hot.astype(jnp.float32) * probs
        weights = (chosen / jnp.sum(chosen, axis=-1, keepdims=True)).astype(jnp.bfloat16)
        combine = match * weights.T[:, None, :]
        mixed = jnp.einsum("ect,ecd->td", combine, returned, preferred_element_type=jnp.float32)
        result = (states.astype(jnp.float32) + mixed).astype(jnp.bfloat16)
        return (result, normed, probs)

    def advance(step, incoming):
        index = step - position
        active = (index >= 0) & (index < micro)
        clipped = jnp.clip(index, 0, micro - 1)
        first = lax.dynamic_index_in_dim(tokens, jnp.minimum(step, micro - 1), 0, keepdims=False)
        states = jnp.where(position == 0, first, incoming)
        hot = lax.dynamic_index_in_dim(hot_all, clipped, 0, keepdims=False)
        result, normed, probs = section_work(states, hot, active)
        passed = from_behind(result, "section", 1)
        return (active, clipped, result, normed, probs, passed)

    steps = micro + sections - 1
    incoming = jnp.zeros((rows, width), jnp.bfloat16)
    outputs = jnp.zeros((micro, rows, width), jnp.bfloat16)
    counts = over_axes(local_counts, DP)
    share = experts * counts.astype(jnp.float32) / (chosen_count * total_rows)

    def loop_before(step, carry):
        received, stored, gradient = carry
        active, clipped, result, normed, probs, passed = advance(step, received)
        contribution = outer_rows(normed, slope_of(probs, share))
        gradient = gradient + jnp.where(active, contribution, jnp.zeros_like(contribution))
        return (passed, place(stored, clipped, result, active), gradient)

    start_carry = (incoming, outputs, jnp.zeros((width, experts), jnp.float32))
    final = lax.fori_loop(0, steps, loop_before, start_carry)
    outputs = final[1]
    grad_rows = summed_on_arrival(final[2].astype(jnp.bfloat16), DP, 0)
    return (outputs[None], grad_rows[None])


def solution(mesh):
    torus = Mesh(mesh.devices.reshape(mesh.shape["section"], 4, 8), ("section", "dp_0", "dp_1"))
    in_specs = (
        P(None, DP, None),
        P("section", None),
        P("section", None, None),
        P("section", DP, None, None),
        P("section", DP, None, None),
        P("section", DP, None, None),
        P("section", None, DP, None),
    )
    out_specs = (P("section", None, DP, None), P("section", DP, None))
    return jax.shard_map(
        on_device, mesh=torus, in_specs=in_specs, out_specs=out_specs, check_vma=False
    )
```

profile of v0, /device:TPU:8, one launch (start us, length us, event | category | flops | bytes accessed | tf_op | source)
XLA Modules:
  0.0 916.3 jit_solution(2309131831117798032)
XLA Ops:
  1.5 8.9 psum.14
  10.4 16.1 %psum.15 = s32[32]{0:T(128)S(1)} all-reduce(s32[32]{0:T(128)S(1)} %psum.14), channel_id=1, replica_groups=mesh['section'=8,'dp_0'=4,'dp_1'=8] {'dp_1'}, use_global_device_ids=true, to_apply=%region_3.0 | all-reduce | flops 32 | bytes 256 | tf_op jit(solution)/shard_map/psum | solution.py:15
  29.3 867.1 %while.19 = (s32[]{:T(128)}, bf16[32,2048]{1,0:T(8,128)(2,1)S(1)}, bf16[4,32,2048]{2,1,0:T(8,128)(2,1)}, f32[2048,32]{0,1:T(8,128)S(1)}, pred[]{:T(512)}, /*inde...) while((s32[]{:T(128)}, bf16[32,2048]{1,0:T(8,128)(2,1)S(1)}, ...), condition=%wide.region_12.13_spmd.clone, body=%wide.region_4.12_spmd.clone.sunk | while | flops 2205553664 | bytes 29838788 | solution.py:148
  37.1 23.3 %all-to-all-done = bf16[32,7,2048]{2,1,0:T(8,128)(2,1)S(1)} async-done(((bf16[32,7,2048]{2,1,0:T(8,128)(2,1)}), bf16[32,7,2048]{2,1,0:T(8,128)(2,1)S(1)}, u32[]{:S(2)}, u32[]{:S(2)}) %all-to-all-start) | async-done | bytes 917536 | tf_op jit(solution)/shard_map/while/body/eval_jaxpr/all_to_all | solution.py:110
  68.8 21.5 %all-to-all-done.1 = bf16[32,7,2048]{2,1,0:T(8,128)(2,1)S(1)} async-done(((bf16[32,7,2048]{2,1,0:T(8,128)(2,1)}), bf16[32,7,2048]{2,1,0:T(8,128)(2,1)S(1)}, u32[]{:S(2)}, u32[]{:S(2)}) %all-to-all-start.1) | async-done | bytes 917536 | tf_op jit(solution)/shard_map/while/body/eval_jaxpr/all_to_all | solution.py:113
  107.1 28.2 %all-to-all-done = bf16[32,7,2048]{2,1,0:T(8,128)(2,1)S(1)} async-done(((bf16[32,7,2048]{2,1,0:T(8,128)(2,1)}), bf16[32,7,2048]{2,1,0:T(8,128)(2,1)S(1)}, u32[]{:S(2)}, u32[]{:S(2)}) %all-to-all-start) | async-done | bytes 917536 | tf_op jit(solution)/shard_map/while/body/eval_jaxpr/all_to_all | solution.py:110
  143.0 26.8 %all-to-all-done.1 = bf16[32,7,2048]{2,1,0:T(8,128)(2,1)S(1)} async-done(((bf16[32,7,2048]{2,1,0:T(8,128)(2,1)}), bf16[32,7,2048]{2,1,0:T(8,128)(2,1)S(1)}, u32[]{:S(2)}, u32[]{:S(2)}) %all-to-all-start.1) | async-done | bytes 917536 | tf_op jit(solution)/shard_map/while/body/eval_jaxpr/all_to_all | solution.py:113
  185.0 8.7 all-to-all-start
  193.8 20.5 %all-to-all-done = bf16[32,7,2048]{2,1,0:T(8,128)(2,1)S(1)} async-done(((bf16[32,7,2048]{2,1,0:T(8,128)(2,1)}), bf16[32,7,2048]{2,1,0:T(8,128)(2,1)S(1)}, u32[]{:S(2)}, u32[]{:S(2)}) %all-to-all-start) | async-done | bytes 917536 | tf_op jit(solution)/shard_map/while/body/eval_jaxpr/all_to_all | solution.py:110
  214.3 8.9 conditional.3
  230.2 16.7 %all-to-all-done.1 = bf16[32,7,2048]{2,1,0:T(8,128)(2,1)S(1)} async-done(((bf16[32,7,2048]{2,1,0:T(8,128)(2,1)}), bf16[32,7,2048]{2,1,0:T(8,128)(2,1)S(1)}, u32[]{:S(2)}, u32[]{:S(2)}) %all-to-all-start.1) | async-done | bytes 917536 | tf_op jit(solution)/shard_map/while/body/eval_jaxpr/all_to_all | solution.py:113
  250.5 17.6 %collective-permute-done = bf16[32,2048]{1,0:T(8,128)(2,1)S(1)} collective-permute-done((bf16[32,2048]{1,0:T(8,128)(2,1)S(1)}, bf16[32,2048]{1,0:T(8,128)(2,1)S(1)}, u32[]{:S(2)}, u32[]{:S(2)}) %collective-permute-start) | collective-permute-done | bytes 131104 | tf_op jit(solution)/shard_map/while/body/eval_jaxpr/ppermute | solution.py:22
  279.8 18.1 %all-to-all-done = bf16[32,7,2048]{2,1,0:T(8,128)(2,1)S(1)} async-done(((bf16[32,7,2048]{2,1,0:T(8,128)(2,1)}), bf16[32,7,2048]{2,1,0:T(8,128)(2,1)S(1)}, u32[]{:S(2)}, u32[]{:S(2)}) %all-to-all-start) | async-done | bytes 917536 | tf_op jit(solution)/shard_map/while/body/eval_jaxpr/all_to_all | solution.py:110
  297.9 8.9 conditional.3
  315.9 16.7 %all-to-all-done.1 = bf16[32,7,2048]{2,1,0:T(8,128)(2,1)S(1)} async-done(((bf16[32,7,2048]{2,1,0:T(8,128)(2,1)}), bf16[32,7,2048]{2,1,0:T(8,128)(2,1)S(1)}, u32[]{:S(2)}, u32[]{:S(2)}) %all-to-all-start.1) | async-done | bytes 917536 | tf_op jit(solution)/shard_map/while/body/eval_jaxpr/all_to_all | solution.py:113
  336.2 18.0 %collective-permute-done = bf16[32,2048]{1,0:T(8,128)(2,1)S(1)} collective-permute-done((bf16[32,2048]{1,0:T(8,128)(2,1)S(1)}, bf16[32,2048]{1,0:T(8,128)(2,1)S(1)}, u32[]{:S(2)}, u32[]{:S(2)}) %collective-permute-start) | collective-permute-done | bytes 131104 | tf_op jit(solution)/shard_map/while/body/eval_jaxpr/ppermute | solution.py:22
  357.6 8.3 all-to-all-start
  365.9 18.1 %all-to-all-done = bf16[32,7,2048]{2,1,0:T(8,128)(2,1)S(1)} async-done(((bf16[32,7,2048]{2,1,0:T(8,128)(2,1)}), bf16[32,7,2048]{2,1,0:T(8,128)(2,1)S(1)}, u32[]{:S(2)}, u32[]{:S(2)}) %all-to-all-start) | async-done | bytes 917536 | tf_op jit(solution)/shard_map/while/body/eval_jaxpr/all_to_all | solution.py:110
  384.0 8.9 conditional.3
  401.9 16.7 %all-to-all-done.1 = bf16[32,7,2048]{2,1,0:T(8,128)(2,1)S(1)} async-done(((bf16[32,7,2048]{2,1,0:T(8,128)(2,1)}), bf16[32,7,2048]{2,1,0:T(8,128)(2,1)S(1)}, u32[]{:S(2)}, u32[]{:S(2)}) %all-to-all-start.1) | async-done | bytes 917536 | tf_op jit(solution)/shard_map/while/body/eval_jaxpr/all_to_all | solution.py:113
  422.2 13.2 %collective-permute-done = bf16[32,2048]{1,0:T(8,128)(2,1)S(1)} collective-permute-done((bf16[32,2048]{1,0:T(8,128)(2,1)S(1)}, bf16[32,2048]{1,0:T(8,128)(2,1)S(1)}, u32[]{:S(2)}, u32[]{:S(2)}) %collective-permute-start) | collective-permute-done | bytes 131104 | tf_op jit(solution)/shard_map/while/body/eval_jaxpr/ppermute | solution.py:22
  444.8 17.5 %all-to-all-done = bf16[32,7,2048]{2,1,0:T(8,128)(2,1)S(1)} async-done(((bf16[32,7,2048]{2,1,0:T(8,128)(2,1)}), bf16[32,7,2048]{2,1,0:T(8,128)(2,1)S(1)}, u32[]{:S(2)}, u32[]{:S(2)}) %all-to-all-start) | async-done | bytes 917536 | tf_op jit(solution)/shard_map/while/body/eval_jaxpr/all_to_all | solution.py:110
  462.3 8.9 conditional.3
  480.4 16.7 %all-to-all-done.1 = bf16[32,7,2048]{2,1,0:T(8,128)(2,1)S(1)} async-done(((bf16[32,7,2048]{2,1,0:T(8,128)(2,1)}), bf16[32,7,2048]{2,1,0:T(8,128)(2,1)S(1)}, u32[]{:S(2)}, u32[]{:S(2)}) %all-to-all-start.1) | async-done | bytes 917536 | tf_op jit(solution)/shard_map/while/body/eval_jaxpr/all_to_all | solution.py:113
  500.7 9.6 %collective-permute-done = bf16[32,2048]{1,0:T(8,128)(2,1)S(1)} collective-permute-done((bf16[32,2048]{1,0:T(8,128)(2,1)S(1)}, bf16[32,2048]{1,0:T(8,128)(2,1)S(1)}, u32[]{:S(2)}, u32[]{:S(2)}) %collective-permute-start) | collective-permute-done | bytes 131104 | tf_op jit(solution)/shard_map/while/body/eval_jaxpr/ppermute | solution.py:22
  522.0 17.8 %all-to-all-done = bf16[32,7,2048]{2,1,0:T(8,128)(2,1)S(1)} async-done(((bf16[32,7,2048]{2,1,0:T(8,128)(2,1)}), bf16[32,7,2048]{2,1,0:T(8,128)(2,1)S(1)}, u32[]{:S(2)}, u32[]{:S(2)}) %all-to-all-start) | async-done | bytes 917536 | tf_op jit(solution)/shard_map/while/body/eval_jaxpr/all_to_all | solution.py:110
  548.8 24.1 %all-to-all-done.1 = bf16[32,7,2048]{2,1,0:T(8,128)(2,1)S(1)} async-done(((bf16[32,7,2048]{2,1,0:T(8,128)(2,1)}), bf16[32,7,2048]{2,1,0:T(8,128)(2,1)S(1)}, u32[]{:S(2)}, u32[]{:S(2)}) %all-to-all-start.1) | async-done | bytes 917536 | tf_op jit(solution)/shard_map/while/body/eval_jaxpr/all_to_all | solution.py:113
  576.5 11.0 %collective-permute-done = bf16[32,2048]{1,0:T(8,128)(2,1)S(1)} collective-permute-done((bf16[32,2048]{1,0:T(8,128)(2,1)S(1)}, bf16[32,2048]{1,0:T(8,128)(2,1)S(1)}, u32[]{:S(2)}, u32[]{:S(2)}) %collective-permute-start) | collective-permute-done | bytes 131104 | tf_op jit(solution)/shard_map/while/body/eval_jaxpr/ppermute | solution.py:22
  591.0 8.3 all-to-all-start
  599.3 18.1 %all-to-all-done = bf16[32,7,2048]{2,1,0:T(8,128)(2,1)S(1)} async-done(((bf16[32,7,2048]{2,1,0:T(8,128)(2,1)}), bf16[32,7,2048]{2,1,0:T(8,128)(2,1)S(1)}, u32[]{:S(2)}, u32[]{:S(2)}) %all-to-all-start) | async-done | bytes 917536 | tf_op jit(solution)/shard_map/while/body/eval_jaxpr/all_to_all | solution.py:110
  618.8 8.4 all-to-all-start.1
  628.6 16.7 %all-to-all-done.1 = bf16[32,7,2048]{2,1,0:T(8,128)(2,1)S(1)} async-done(((bf16[32,7,2048]{2,1,0:T(8,128)(2,1)}), bf16[32,7,2048]{2,1,0:T(8,128)(2,1)S(1)}, u32[]{:S(2)}, u32[]{:S(2)}) %all-to-all-start.1) | async-done | bytes 917536 | tf_op jit(solution)/shard_map/while/body/eval_jaxpr/all_to_all | solution.py:113
  648.9 15.8 %collective-permute-done = bf16[32,2048]{1,0:T(8,128)(2,1)S(1)} collective-permute-done((bf16[32,2048]{1,0:T(8,128)(2,1)S(1)}, bf16[32,2048]{1,0:T(8,128)(2,1)S(1)}, u32[]{:S(2)}, u32[]{:S(2)}) %collective-permute-start) | collective-permute-done | bytes 131104 | tf_op jit(solution)/shard_map/while/body/eval_jaxpr/ppermute | solution.py:22
  668.2 8.3 all-to-all-start
  676.5 20.6 %all-to-all-done = bf16[32,7,2048]{2,1,0:T(8,128)(2,1)S(1)} async-done(((bf16[32,7,2048]{2,1,0:T(8,128)(2,1)}), bf16[32,7,2048]{2,1,0:T(8,128)(2,1)S(1)}, u32[]{:S(2)}, u32[]{:S(2)}) %all-to-all-start) | async-done | bytes 917536 | tf_op jit(solution)/shard_map/while/body/eval_jaxpr/all_to_all | solution.py:110
  698.5 10.1 %all-to-all-start.1 = ((bf16[32,7,2048]{2,1,0:T(8,128)(2,1)}), bf16[32,7,2048]{2,1,0:T(8,128)(2,1)S(1)}, u32[]{:S(2)}, u32[]{:S(2)}) async-start(bf16[32,7,2048]{2,1,0:T(8,128)(2,1)} %reshape.59), calls=%async_computation.1 | async-start | bytes 2097152 | tf_op jit(solution)/shard_map/while/body/eval_jaxpr/all_to_all | solution.py:113
  710.1 16.7 %all-to-all-done.1 = bf16[32,7,2048]{2,1,0:T(8,128)(2,1)S(1)} async-done(((bf16[32,7,2048]{2,1,0:T(8,128)(2,1)}), bf16[32,7,2048]{2,1,0:T(8,128)(2,1)S(1)}, u32[]{:S(2)}, u32[]{:S(2)}) %all-to-all-start.1) | async-done | bytes 917536 | tf_op jit(solution)/shard_map/while/body/eval_jaxpr/all_to_all | solution.py:113
  730.4 11.5 %collective-permute-done = bf16[32,2048]{1,0:T(8,128)(2,1)S(1)} collective-permute-done((bf16[32,2048]{1,0:T(8,128)(2,1)S(1)}, bf16[32,2048]{1,0:T(8,128)(2,1)S(1)}, u32[]{:S(2)}, u32[]{:S(2)}) %collective-permute-start) | collective-permute-done | bytes 131104 | tf_op jit(solution)/shard_map/while/body/eval_jaxpr/ppermute | solution.py:22
  745.4 8.3 all-to-all-start
  753.7 18.1 %all-to-all-done = bf16[32,7,2048]{2,1,0:T(8,128)(2,1)S(1)} async-done(((bf16[32,7,2048]{2,1,0:T(8,128)(2,1)}), bf16[32,7,2048]{2,1,0:T(8,128)(2,1)S(1)}, u32[]{:S(2)}, u32[]{:S(2)}) %all-to-all-start) | async-done | bytes 917536 | tf_op jit(solution)/shard_map/while/body/eval_jaxpr/all_to_all | solution.py:110
  782.9 16.7 %all-to-all-done.1 = bf16[32,7,2048]{2,1,0:T(8,128)(2,1)S(1)} async-done(((bf16[32,7,2048]{2,1,0:T(8,128)(2,1)}), bf16[32,7,2048]{2,1,0:T(8,128)(2,1)S(1)}, u32[]{:S(2)}, u32[]{:S(2)}) %all-to-all-start.1) | async-done | bytes 917536 | tf_op jit(solution)/shard_map/while/body/eval_jaxpr/all_to_all | solution.py:113
  803.2 16.0 %collective-permute-done = bf16[32,2048]{1,0:T(8,128)(2,1)S(1)} collective-permute-done((bf16[32,2048]{1,0:T(8,128)(2,1)S(1)}, bf16[32,2048]{1,0:T(8,128)(2,1)S(1)}, u32[]{:S(2)}, u32[]{:S(2)}) %collective-permute-start) | collective-permute-done | bytes 131104 | tf_op jit(solution)/shard_map/while/body/eval_jaxpr/ppermute | solution.py:22
  822.6 8.3 all-to-all-start
  830.9 20.9 %all-to-all-done = bf16[32,7,2048]{2,1,0:T(8,128)(2,1)S(1)} async-done(((bf16[32,7,2048]{2,1,0:T(8,128)(2,1)}), bf16[32,7,2048]{2,1,0:T(8,128)(2,1)S(1)}, u32[]{:S(2)}, u32[]{:S(2)}) %all-to-all-start) | async-done | bytes 917536 | tf_op jit(solution)/shard_map/while/body/eval_jaxpr/all_to_all | solution.py:110
  853.3 9.8 %all-to-all-start.1 = ((bf16[32,7,2048]{2,1,0:T(8,128)(2,1)}), bf16[32,7,2048]{2,1,0:T(8,128)(2,1)S(1)}, u32[]{:S(2)}, u32[]{:S(2)}) async-start(bf16[32,7,2048]{2,1,0:T(8,128)(2,1)} %reshape.59), calls=%async_computation.1 | async-start | bytes 2097152 | tf_op jit(solution)/shard_map/while/body/eval_jaxpr/all_to_all | solution.py:113
  864.6 16.7 %all-to-all-done.1 = bf16[32,7,2048]{2,1,0:T(8,128)(2,1)S(1)} async-done(((bf16[32,7,2048]{2,1,0:T(8,128)(2,1)}), bf16[32,7,2048]{2,1,0:T(8,128)(2,1)S(1)}, u32[]{:S(2)}, u32[]{:S(2)}) %all-to-all-start.1) | async-done | bytes 917536 | tf_op jit(solution)/shard_map/while/body/eval_jaxpr/all_to_all | solution.py:113
  884.9 11.6 %collective-permute-done = bf16[32,2048]{1,0:T(8,128)(2,1)S(1)} collective-permute-done((bf16[32,2048]{1,0:T(8,128)(2,1)S(1)}, bf16[32,2048]{1,0:T(8,128)(2,1)S(1)}, u32[]{:S(2)}, u32[]{:S(2)}) %collective-permute-start) | collective-permute-done | bytes 131104 | tf_op jit(solution)/shard_map/while/body/eval_jaxpr/ppermute | solution.py:22
  897.0 18.4 %all_to_all.29 = bf16[32,2,1024]{2,1,0:T(2,128)(2,1)S(1)} all-to-all(bf16[32,2,1024]{2,1,0:T(2,128)(2,1)S(1)} %reshape.56), channel_id=1, replica_groups=mesh['section'=8,'dp_0'=4,'dp_1'=8] {'dp_0','dp_1'}, dimensions={0} | all-to-all | bytes 262144 | tf_op jit(solution)/shard_map/all_to_all | solution.py:33
  (308 shorter events, 242.0 us)
Async XLA Ops:
  32.9 27.5 %all-to-all-start = ((bf16[32,7,2048]{2,1,0:T(8,128)(2,1)}), bf16[32,7,2048]{2,1,0:T(8,128)(2,1)S(1)}, u32[]{:S(2)}, u32[]{:S(2)}) async-start(bf16[32,7,2048]{2,1,0:T(8,128)(2,1)} %copy.82), calls=%async_computation | async-start | bytes 2097152 | tf_op jit(solution)/shard_map/while/body/eval_jaxpr/all_to_all | solution.py:110
  61.8 28.5 %all-to-all-start.1 = ((bf16[32,7,2048]{2,1,0:T(8,128)(2,1)}), bf16[32,7,2048]{2,1,0:T(8,128)(2,1)S(1)}, u32[]{:S(2)}, u32[]{:S(2)}) async-start(bf16[32,7,2048]{2,1,0:T(8,128)(2,1)} %reshape.59), calls=%async_computation.1 | async-start | bytes 2097152 | tf_op jit(solution)/shard_map/while/body/eval_jaxpr/all_to_all | solution.py:113
  91.6 6.3 collective-permute-start
  101.4 33.9 %all-to-all-start = ((bf16[32,7,2048]{2,1,0:T(8,128)(2,1)}), bf16[32,7,2048]{2,1,0:T(8,128)(2,1)S(1)}, u32[]{:S(2)}, u32[]{:S(2)}) async-start(bf16[32,7,2048]{2,1,0:T(8,128)(2,1)} %copy.82), calls=%async_computation | async-start | bytes 2097152 | tf_op jit(solution)/shard_map/while/body/eval_jaxpr/all_to_all | solution.py:110
  136.7 33.2 %all-to-all-start.1 = ((bf16[32,7,2048]{2,1,0:T(8,128)(2,1)}), bf16[32,7,2048]{2,1,0:T(8,128)(2,1)S(1)}, u32[]{:S(2)}, u32[]{:S(2)}) async-start(bf16[32,7,2048]{2,1,0:T(8,128)(2,1)} %reshape.59), calls=%async_computation.1 | async-start | bytes 2097152 | tf_op jit(solution)/shard_map/while/body/eval_jaxpr/all_to_all | solution.py:113
  171.3 10.3 %collective-permute-start = (bf16[32,2048]{1,0:T(8,128)(2,1)S(1)}, bf16[32,2048]{1,0:T(8,128)(2,1)S(1)}, u32[]{:S(2)}, u32[]{:S(2)}) collective-permute-start(bf16[32,2048]{1,0:T(8,128)(2,1)S(1)} %get-tuple-element.521), channel_id=1, source_target_pairs={{0,32},{32,64},{64,96},{96,128},{128,160},{160,192},{192,224},{1,3... | collective-permute-start | bytes 393224 | tf_op jit(solution)/shard_map/while/body/eval_jaxpr/ppermute | solution.py:22
  185.0 29.2 %all-to-all-start = ((bf16[32,7,2048]{2,1,0:T(8,128)(2,1)}), bf16[32,7,2048]{2,1,0:T(8,128)(2,1)S(1)}, u32[]{:S(2)}, u32[]{:S(2)}) async-start(bf16[32,7,2048]{2,1,0:T(8,128)(2,1)} %copy.82), calls=%async_computation | async-start | bytes 2097152 | tf_op jit(solution)/shard_map/while/body/eval_jaxpr/all_to_all | solution.py:110
  224.5 22.4 %all-to-all-start.1 = ((bf16[32,7,2048]{2,1,0:T(8,128)(2,1)}), bf16[32,7,2048]{2,1,0:T(8,128)(2,1)S(1)}, u32[]{:S(2)}, u32[]{:S(2)}) async-start(bf16[32,7,2048]{2,1,0:T(8,128)(2,1)} %reshape.59), calls=%async_computation.1 | async-start | bytes 2097152 | tf_op jit(solution)/shard_map/while/body/eval_jaxpr/all_to_all | solution.py:113
  248.3 19.8 %collective-permute-start = (bf16[32,2048]{1,0:T(8,128)(2,1)S(1)}, bf16[32,2048]{1,0:T(8,128)(2,1)S(1)}, u32[]{:S(2)}, u32[]{:S(2)}) collective-permute-start(bf16[32,2048]{1,0:T(8,128)(2,1)S(1)} %get-tuple-element.521), channel_id=1, source_target_pairs={{0,32},{32,64},{64,96},{96,128},{128,160},{160,192},{192,224},{1,3... | collective-permute-start | bytes 393224 | tf_op jit(solution)/shard_map/while/body/eval_jaxpr/ppermute | solution.py:22
  271.5 26.4 %all-to-all-start = ((bf16[32,7,2048]{2,1,0:T(8,128)(2,1)}), bf16[32,7,2048]{2,1,0:T(8,128)(2,1)S(1)}, u32[]{:S(2)}, u32[]{:S(2)}) async-start(bf16[32,7,2048]{2,1,0:T(8,128)(2,1)} %copy.82), calls=%async_computation | async-start | bytes 2097152 | tf_op jit(solution)/shard_map/while/body/eval_jaxpr/all_to_all | solution.py:110
  308.2 24.4 %all-to-all-start.1 = ((bf16[32,7,2048]{2,1,0:T(8,128)(2,1)}), bf16[32,7,2048]{2,1,0:T(8,128)(2,1)S(1)}, u32[]{:S(2)}, u32[]{:S(2)}) async-start(bf16[32,7,2048]{2,1,0:T(8,128)(2,1)} %reshape.59), calls=%async_computation.1 | async-start | bytes 2097152 | tf_op jit(solution)/shard_map/while/body/eval_jaxpr/all_to_all | solution.py:113
  333.9 20.2 %collective-permute-start = (bf16[32,2048]{1,0:T(8,128)(2,1)S(1)}, bf16[32,2048]{1,0:T(8,128)(2,1)S(1)}, u32[]{:S(2)}, u32[]{:S(2)}) collective-permute-start(bf16[32,2048]{1,0:T(8,128)(2,1)S(1)} %get-tuple-element.521), channel_id=1, source_target_pairs={{0,32},{32,64},{64,96},{96,128},{128,160},{160,192},{192,224},{1,3... | collective-permute-start | bytes 393224 | tf_op jit(solution)/shard_map/while/body/eval_jaxpr/ppermute | solution.py:22
  357.6 26.4 %all-to-all-start = ((bf16[32,7,2048]{2,1,0:T(8,128)(2,1)}), bf16[32,7,2048]{2,1,0:T(8,128)(2,1)S(1)}, u32[]{:S(2)}, u32[]{:S(2)}) async-start(bf16[32,7,2048]{2,1,0:T(8,128)(2,1)} %copy.82), calls=%async_computation | async-start | bytes 2097152 | tf_op jit(solution)/shard_map/while/body/eval_jaxpr/all_to_all | solution.py:110
  394.2 24.4 %all-to-all-start.1 = ((bf16[32,7,2048]{2,1,0:T(8,128)(2,1)}), bf16[32,7,2048]{2,1,0:T(8,128)(2,1)S(1)}, u32[]{:S(2)}, u32[]{:S(2)}) async-start(bf16[32,7,2048]{2,1,0:T(8,128)(2,1)} %reshape.59), calls=%async_computation.1 | async-start | bytes 2097152 | tf_op jit(solution)/shard_map/while/body/eval_jaxpr/all_to_all | solution.py:113
  420.0 15.4 %collective-permute-start = (bf16[32,2048]{1,0:T(8,128)(2,1)S(1)}, bf16[32,2048]{1,0:T(8,128)(2,1)S(1)}, u32[]{:S(2)}, u32[]{:S(2)}) collective-permute-start(bf16[32,2048]{1,0:T(8,128)(2,1)S(1)} %get-tuple-element.521), channel_id=1, source_target_pairs={{0,32},{32,64},{64,96},{96,128},{128,160},{160,192},{192,224},{1,3... | collective-permute-start | bytes 393224 | tf_op jit(solution)/shard_map/while/body/eval_jaxpr/ppermute | solution.py:22
  438.8 23.5 %all-to-all-start = ((bf16[32,7,2048]{2,1,0:T(8,128)(2,1)}), bf16[32,7,2048]{2,1,0:T(8,128)(2,1)S(1)}, u32[]{:S(2)}, u32[]{:S(2)}) async-start(bf16[32,7,2048]{2,1,0:T(8,128)(2,1)} %copy.82), calls=%async_computation | async-start | bytes 2097152 | tf_op jit(solution)/shard_map/while/body/eval_jaxpr/all_to_all | solution.py:110
  472.5 24.5 %all-to-all-start.1 = ((bf16[32,7,2048]{2,1,0:T(8,128)(2,1)}), bf16[32,7,2048]{2,1,0:T(8,128)(2,1)S(1)}, u32[]{:S(2)}, u32[]{:S(2)}) async-start(bf16[32,7,2048]{2,1,0:T(8,128)(2,1)} %reshape.59), calls=%async_computation.1 | async-start | bytes 2097152 | tf_op jit(solution)/shard_map/while/body/eval_jaxpr/all_to_all | solution.py:113
  498.4 11.9 %collective-permute-start = (bf16[32,2048]{1,0:T(8,128)(2,1)S(1)}, bf16[32,2048]{1,0:T(8,128)(2,1)S(1)}, u32[]{:S(2)}, u32[]{:S(2)}) collective-permute-start(bf16[32,2048]{1,0:T(8,128)(2,1)S(1)} %get-tuple-element.521), channel_id=1, source_target_pairs={{0,32},{32,64},{64,96},{96,128},{128,160},{160,192},{192,224},{1,3... | collective-permute-start | bytes 393224 | tf_op jit(solution)/shard_map/while/body/eval_jaxpr/ppermute | solution.py:22
  513.8 26.1 %all-to-all-start = ((bf16[32,7,2048]{2,1,0:T(8,128)(2,1)}), bf16[32,7,2048]{2,1,0:T(8,128)(2,1)S(1)}, u32[]{:S(2)}, u32[]{:S(2)}) async-start(bf16[32,7,2048]{2,1,0:T(8,128)(2,1)} %copy.82), calls=%async_computation | async-start | bytes 2097152 | tf_op jit(solution)/shard_map/while/body/eval_jaxpr/all_to_all | solution.py:110
  541.2 31.6 %all-to-all-start.1 = ((bf16[32,7,2048]{2,1,0:T(8,128)(2,1)}), bf16[32,7,2048]{2,1,0:T(8,128)(2,1)S(1)}, u32[]{:S(2)}, u32[]{:S(2)}) async-start(bf16[32,7,2048]{2,1,0:T(8,128)(2,1)} %reshape.59), calls=%async_computation.1 | async-start | bytes 2097152 | tf_op jit(solution)/shard_map/while/body/eval_jaxpr/all_to_all | solution.py:113
  574.3 13.2 %collective-permute-start = (bf16[32,2048]{1,0:T(8,128)(2,1)S(1)}, bf16[32,2048]{1,0:T(8,128)(2,1)S(1)}, u32[]{:S(2)}, u32[]{:S(2)}) collective-permute-start(bf16[32,2048]{1,0:T(8,128)(2,1)S(1)} %get-tuple-element.521), channel_id=1, source_target_pairs={{0,32},{32,64},{64,96},{96,128},{128,160},{160,192},{192,224},{1,3... | collective-permute-start | bytes 393224 | tf_op jit(solution)/shard_map/while/body/eval_jaxpr/ppermute | solution.py:22
  591.0 26.4 %all-to-all-start = ((bf16[32,7,2048]{2,1,0:T(8,128)(2,1)}), bf16[32,7,2048]{2,1,0:T(8,128)(2,1)S(1)}, u32[]{:S(2)}, u32[]{:S(2)}) async-start(bf16[32,7,2048]{2,1,0:T(8,128)(2,1)} %copy.82), calls=%async_computation | async-start | bytes 2097152 | tf_op jit(solution)/shard_map/while/body/eval_jaxpr/all_to_all | solution.py:110
  618.8 26.5 %all-to-all-start.1 = ((bf16[32,7,2048]{2,1,0:T(8,128)(2,1)}), bf16[32,7,2048]{2,1,0:T(8,128)(2,1)S(1)}, u32[]{:S(2)}, u32[]{:S(2)}) async-start(bf16[32,7,2048]{2,1,0:T(8,128)(2,1)} %reshape.59), calls=%async_computation.1 | async-start | bytes 2097152 | tf_op jit(solution)/shard_map/while/body/eval_jaxpr/all_to_all | solution.py:113
  646.7 18.1 %collective-permute-start = (bf16[32,2048]{1,0:T(8,128)(2,1)S(1)}, bf16[32,2048]{1,0:T(8,128)(2,1)S(1)}, u32[]{:S(2)}, u32[]{:S(2)}) collective-permute-start(bf16[32,2048]{1,0:T(8,128)(2,1)S(1)} %get-tuple-element.521), channel_id=1, source_target_pairs={{0,32},{32,64},{64,96},{96,128},{128,160},{160,192},{192,224},{1,3... | collective-permute-start | bytes 393224 | tf_op jit(solution)/shard_map/while/body/eval_jaxpr/ppermute | solution.py:22
  668.2 28.9 %all-to-all-start = ((bf16[32,7,2048]{2,1,0:T(8,128)(2,1)}), bf16[32,7,2048]{2,1,0:T(8,128)(2,1)S(1)}, u32[]{:S(2)}, u32[]{:S(2)}) async-start(bf16[32,7,2048]{2,1,0:T(8,128)(2,1)} %copy.82), calls=%async_computation | async-start | bytes 2097152 | tf_op jit(solution)/shard_map/while/body/eval_jaxpr/all_to_all | solution.py:110
  698.5 28.3 %all-to-all-start.1 = ((bf16[32,7,2048]{2,1,0:T(8,128)(2,1)}), bf16[32,7,2048]{2,1,0:T(8,128)(2,1)S(1)}, u32[]{:S(2)}, u32[]{:S(2)}) async-start(bf16[32,7,2048]{2,1,0:T(8,128)(2,1)} %reshape.59), calls=%async_computation.1 | async-start | bytes 2097152 | tf_op jit(solution)/shard_map/while/body/eval_jaxpr/all_to_all | solution.py:113
  728.2 13.8 %collective-permute-start = (bf16[32,2048]{1,0:T(8,128)(2,1)S(1)}, bf16[32,2048]{1,0:T(8,128)(2,1)S(1)}, u32[]{:S(2)}, u32[]{:S(2)}) collective-permute-start(bf16[32,2048]{1,0:T(8,128)(2,1)S(1)} %get-tuple-element.521), channel_id=1, source_target_pairs={{0,32},{32,64},{64,96},{96,128},{128,160},{160,192},{192,224},{1,3... | collective-permute-start | bytes 393224 | tf_op jit(solution)/shard_map/while/body/eval_jaxpr/ppermute | solution.py:22
  745.4 26.4 %all-to-all-start = ((bf16[32,7,2048]{2,1,0:T(8,128)(2,1)}), bf16[32,7,2048]{2,1,0:T(8,128)(2,1)S(1)}, u32[]{:S(2)}, u32[]{:S(2)}) async-start(bf16[32,7,2048]{2,1,0:T(8,128)(2,1)} %copy.82), calls=%async_computation | async-start | bytes 2097152 | tf_op jit(solution)/shard_map/while/body/eval_jaxpr/all_to_all | solution.py:110
  773.2 26.3 %all-to-all-start.1 = ((bf16[32,7,2048]{2,1,0:T(8,128)(2,1)}), bf16[32,7,2048]{2,1,0:T(8,128)(2,1)S(1)}, u32[]{:S(2)}, u32[]{:S(2)}) async-start(bf16[32,7,2048]{2,1,0:T(8,128)(2,1)} %reshape.59), calls=%async_computation.1 | async-start | bytes 2097152 | tf_op jit(solution)/shard_map/while/body/eval_jaxpr/all_to_all | solution.py:113
  800.9 18.3 %collective-permute-start = (bf16[32,2048]{1,0:T(8,128)(2,1)S(1)}, bf16[32,2048]{1,0:T(8,128)(2,1)S(1)}, u32[]{:S(2)}, u32[]{:S(2)}) collective-permute-start(bf16[32,2048]{1,0:T(8,128)(2,1)S(1)} %get-tuple-element.521), channel_id=1, source_target_pairs={{0,32},{32,64},{64,96},{96,128},{128,160},{160,192},{192,224},{1,3... | collective-permute-start | bytes 393224 | tf_op jit(solution)/shard_map/while/body/eval_jaxpr/ppermute | solution.py:22
  822.6 29.2 %all-to-all-start = ((bf16[32,7,2048]{2,1,0:T(8,128)(2,1)}), bf16[32,7,2048]{2,1,0:T(8,128)(2,1)S(1)}, u32[]{:S(2)}, u32[]{:S(2)}) async-start(bf16[32,7,2048]{2,1,0:T(8,128)(2,1)} %copy.82), calls=%async_computation | async-start | bytes 2097152 | tf_op jit(solution)/shard_map/while/body/eval_jaxpr/all_to_all | solution.py:110
  853.3 27.9 %all-to-all-start.1 = ((bf16[32,7,2048]{2,1,0:T(8,128)(2,1)}), bf16[32,7,2048]{2,1,0:T(8,128)(2,1)S(1)}, u32[]{:S(2)}, u32[]{:S(2)}) async-start(bf16[32,7,2048]{2,1,0:T(8,128)(2,1)} %reshape.59), calls=%async_computation.1 | async-start | bytes 2097152 | tf_op jit(solution)/shard_map/while/body/eval_jaxpr/all_to_all | solution.py:113
  882.6 13.8 %collective-permute-start = (bf16[32,2048]{1,0:T(8,128)(2,1)S(1)}, bf16[32,2048]{1,0:T(8,128)(2,1)S(1)}, u32[]{:S(2)}, u32[]{:S(2)}) collective-permute-start(bf16[32,2048]{1,0:T(8,128)(2,1)S(1)} %get-tuple-element.521), channel_id=1, source_target_pairs={{0,32},{32,64},{64,96},{96,128},{128,160},{160,192},{192,224},{1,3... | collective-permute-start | bytes 393224 | tf_op jit(solution)/shard_map/while/body/eval_jaxpr/ppermute | solution.py:22
where the time goes:
time: 920 us; the launch traced here: 916 us
  waiting for transfers between devices  563 us (61%)
  starting transfers between devices  180 us (20%)
  matrix products  62.1 us (7%)
  local copies, waits for them, and re-layouts  50.6 us (6%)
  blocking collectives  43.4 us (5%)
  other arithmetic  15.4 us (2%)
    all_to_all x11, waiting for transfers between devices, section_work(): received = lax.all_to_all(sent, DP, split_axis=0, concat_axis=0, tiled=True)  221 us
    all_to_all x11, waiting for transfers between devices, section_work(): lax.all_to_all(produced.reshape(received.shape), DP, split_axis=0, concat...  206 us
    ppermute x11, waiting for transfers between devices, from_behind(): lax.ppermute(value, axis, [(source, source + steps) for source in range(i...  136 us
    all_to_all x11, starting transfers between devices, section_work(): received = lax.all_to_all(sent, DP, split_axis=0, concat_axis=0, tiled=True)  82.5 us
    all_to_all x11, starting transfers between devices, section_work(): lax.all_to_all(produced.reshape(received.shape), DP, split_axis=0, concat...  76.1 us
    psum x2, blocking collectives, over_axes(): shard = lax.psum(shard, axis)  25 us
    ppermute x11, starting transfers between devices, from_behind(): lax.ppermute(value, axis, [(source, source + steps) for source in range(i...  21 us
    dot_general x4, matrix products, expert_ffn(): jnp.dot(hidden, w_down, preferred_element_type=jnp.float32)  19.9 us
  transfers between devices with their start and end apart: 33, of which 33 were waited for; matrix products, arithmetic and copies ran while one was open for 2% of the time, Pallas kernels for 0%

commit v1 on v0

--- a/solution.py
+++ b/solution.py
@@ -87,13 +87,15 @@
     hot_all = (routing[0][..., None] == expert_ids).astype(jnp.int32).sum(axis=2)
     local_counts = jnp.sum(hot_all, axis=(0, 1))
     slot_ids = jnp.arange(slots, dtype=jnp.int32)
+    row_ids = jnp.arange(rows, dtype=jnp.int32)
+    before = (row_ids[:, None] > row_ids[None, :]).astype(jnp.bfloat16)
 
     def section_work(states, hot, active):
         normed = normalize(states, gain)
         logits = jnp.dot(normed, w_router, preferred_element_type=jnp.float32)
         exps = jnp.exp(logits)
         probs = exps / jnp.sum(exps, axis=-1, keepdims=True)
-        rank = jnp.cumsum(hot, axis=0) - hot
+        rank = jnp.dot(before, hot.astype(jnp.bfloat16), preferred_element_type=jnp.float32).astype(jnp.int32)
         match = ((hot.T[:, None, :] == 1) & (rank.T[:, None, :] == slot_ids[None, :, None])).astype(
             jnp.bfloat16
         )

time: 920 us -> 920 us (level)
  no operation moved by 1% of the time
where the time goes in v1:
time: 920 us; the launch traced here: 916 us
  waiting for transfers between devices  563 us (61%)
  starting transfers between devices  180 us (20%)
  matrix products  63.6 us (7%)
  local copies, waits for them, and re-layouts  49.8 us (5%)
  blocking collectives  43.4 us (5%)
  other arithmetic  14.7 us (2%)
    all_to_all x11, waiting for transfers between devices, section_work(): received = lax.all_to_all(sent, DP, split_axis=0, concat_axis=0, tiled=True)  221 us
    all_to_all x11, waiting for transfers between devices, section_work(): lax.all_to_all(produced.reshape(received.shape), DP, split_axis=0, concat...  206 us
    ppermute x11, waiting for transfers between devices, from_behind(): lax.ppermute(value, axis, [(source, source + steps) for source in range(i...  136 us
    all_to_all x11, starting transfers between devices, section_work(): received = lax.all_to_all(sent, DP, split_axis=0, concat_axis=0, tiled=True)  82.5 us
    all_to_all x11, starting transfers between devices, section_work(): lax.all_to_all(produced.reshape(received.shape), DP, split_axis=0, concat...  76.3 us
    psum x2, blocking collectives, over_axes(): shard = lax.psum(shard, axis)  25 us
    ppermute x11, starting transfers between devices, from_behind(): lax.ppermute(value, axis, [(source, source + steps) for source in range(i...  21 us
    dot_general x4, matrix products, expert_ffn(): jnp.dot(hidden, w_down, preferred_element_type=jnp.float32)  19.9 us
  transfers between devices with their start and end apart: 33, of which 33 were waited for; matrix products, arithmetic and copies ran while one was open for 2% of the time, Pallas kernels for 0%

profile of v1, /device:TPU:8, one launch (start us, length us, event | category | flops | bytes accessed | tf_op | source)
XLA Modules:
  0.0 916.3 jit_solution(12094145917065917706)
XLA Ops:
  1.5 8.9 psum.14
  10.4 16.1 %psum.15 = s32[32]{0:T(128)S(1)} all-reduce(s32[32]{0:T(128)S(1)} %psum.14), channel_id=1, replica_groups=mesh['section'=8,'dp_0'=4,'dp_1'=8] {'dp_1'}, use_global_device_ids=true, to_apply=%region_3.0 | all-reduce | flops 32 | bytes 256 | tf_op jit(solution)/shard_map/psum | solution.py:15
  29.3 867.1 %while.19 = (s32[]{:T(128)}, bf16[32,2048]{1,0:T(8,128)(2,1)S(1)}, bf16[4,32,2048]{2,1,0:T(8,128)(2,1)}, f32[2048,32]{0,1:T(8,128)S(1)}, pred[]{:T(512)}, /*inde...) while((s32[]{:T(128)}, bf16[32,2048]{1,0:T(8,128)(2,1)S(1)}, ...), condition=%wide.region_11.12_spmd.clone, body=%wide.region_4.11_spmd.clone.sunk | while | flops 2205590528 | bytes 29810108 | solution.py:150
  37.0 23.3 %all-to-all-done = bf16[32,7,2048]{2,1,0:T(8,128)(2,1)S(1)} async-done(((bf16[32,7,2048]{2,1,0:T(8,128)(2,1)}), bf16[32,7,2048]{2,1,0:T(8,128)(2,1)S(1)}, u32[]{:S(2)}, u32[]{:S(2)}) %all-to-all-start) | async-done | bytes 917536 | tf_op jit(solution)/shard_map/while/body/eval_jaxpr/all_to_all | solution.py:112
  68.7 21.5 %all-to-all-done.1 = bf16[32,7,2048]{2,1,0:T(8,128)(2,1)S(1)} async-done(((bf16[32,7,2048]{2,1,0:T(8,128)(2,1)}), bf16[32,7,2048]{2,1,0:T(8,128)(2,1)S(1)}, u32[]{:S(2)}, u32[]{:S(2)}) %all-to-all-start.1) | async-done | bytes 917536 | tf_op jit(solution)/shard_map/while/body/eval_jaxpr/all_to_all | solution.py:115
  107.0 28.2 %all-to-all-done = bf16[32,7,2048]{2,1,0:T(8,128)(2,1)S(1)} async-done(((bf16[32,7,2048]{2,1,0:T(8,128)(2,1)}), bf16[32,7,2048]{2,1,0:T(8,128)(2,1)S(1)}, u32[]{:S(2)}, u32[]{:S(2)}) %all-to-all-start) | async-done | bytes 917536 | tf_op jit(solution)/shard_map/while/body/eval_jaxpr/all_to_all | solution.py:112
  143.0 26.8 %all-to-all-done.1 = bf16[32,7,2048]{2,1,0:T(8,128)(2,1)S(1)} async-done(((bf16[32,7,2048]{2,1,0:T(8,128)(2,1)}), bf16[32,7,2048]{2,1,0:T(8,128)(2,1)S(1)}, u32[]{:S(2)}, u32[]{:S(2)}) %all-to-all-start.1) | async-done | bytes 917536 | tf_op jit(solution)/shard_map/while/body/eval_jaxpr/all_to_all | solution.py:115
  185.0 8.7 all-to-all-start
  193.8 20.4 %all-to-all-done = bf16[32,7,2048]{2,1,0:T(8,128)(2,1)S(1)} async-done(((bf16[32,7,2048]{2,1,0:T(8,128)(2,1)}), bf16[32,7,2048]{2,1,0:T(8,128)(2,1)S(1)}, u32[]{:S(2)}, u32[]{:S(2)}) %all-to-all-start) | async-done | bytes 917536 | tf_op jit(solution)/shard_map/while/body/eval_jaxpr/all_to_all | solution.py:112
  214.2 8.9 conditional.3
  230.2 16.7 %all-to-all-done.1 = bf16[32,7,2048]{2,1,0:T(8,128)(2,1)S(1)} async-done(((bf16[32,7,2048]{2,1,0:T(8,128)(2,1)}), bf16[32,7,2048]{2,1,0:T(8,128)(2,1)S(1)}, u32[]{:S(2)}, u32[]{:S(2)}) %all-to-all-start.1) | async-done | bytes 917536 | tf_op jit(solution)/shard_map/while/body/eval_jaxpr/all_to_all | solution.py:115
  250.5 17.6 %collective-permute-done = bf16[32,2048]{1,0:T(8,128)(2,1)S(1)} collective-permute-done((bf16[32,2048]{1,0:T(8,128)(2,1)S(1)}, bf16[32,2048]{1,0:T(8,128)(2,1)S(1)}, u32[]{:S(2)}, u32[]{:S(2)}) %collective-permute-start) | collective-permute-done | bytes 131104 | tf_op jit(solution)/shard_map/while/body/eval_jaxpr/ppermute | solution.py:22
  271.6 8.3 all-to-all-start
  279.9 18.1 %all-to-all-done = bf16[32,7,2048]{2,1,0:T(8,128)(2,1)S(1)} async-done(((bf16[32,7,2048]{2,1,0:T(8,128)(2,1)}), bf16[32,7,2048]{2,1,0:T(8,128)(2,1)S(1)}, u32[]{:S(2)}, u32[]{:S(2)}) %all-to-all-start) | async-done | bytes 917536 | tf_op jit(solution)/shard_map/while/body/eval_jaxpr/all_to_all | solution.py:112
  298.0 8.9 conditional.3
  315.9 16.7 %all-to-all-done.1 = bf16[32,7,2048]{2,1,0:T(8,128)(2,1)S(1)} async-done(((bf16[32,7,2048]{2,1,0:T(8,128)(2,1)}), bf16[32,7,2048]{2,1,0:T(8,128)(2,1)S(1)}, u32[]{:S(2)}, u32[]{:S(2)}) %all-to-all-start.1) | async-done | bytes 917536 | tf_op jit(solution)/shard_map/while/body/eval_jaxpr/all_to_all | solution.py:115
  336.2 18.0 %collective-permute-done = bf16[32,2048]{1,0:T(8,128)(2,1)S(1)} collective-permute-done((bf16[32,2048]{1,0:T(8,128)(2,1)S(1)}, bf16[32,2048]{1,0:T(8,128)(2,1)S(1)}, u32[]{:S(2)}, u32[]{:S(2)}) %collective-permute-start) | collective-permute-done | bytes 131104 | tf_op jit(solution)/shard_map/while/body/eval_jaxpr/ppermute | solution.py:22
  365.9 18.1 %all-to-all-done = bf16[32,7,2048]{2,1,0:T(8,128)(2,1)S(1)} async-done(((bf16[32,7,2048]{2,1,0:T(8,128)(2,1)}), bf16[32,7,2048]{2,1,0:T(8,128)(2,1)S(1)}, u32[]{:S(2)}, u32[]{:S(2)}) %all-to-all-start) | async-done | bytes 917536 | tf_op jit(solution)/shard_map/while/body/eval_jaxpr/all_to_all | solution.py:112
  384.0 8.9 conditional.3
  402.0 16.7 %all-to-all-done.1 = bf16[32,7,2048]{2,1,0:T(8,128)(2,1)S(1)} async-done(((bf16[32,7,2048]{2,1,0:T(8,128)(2,1)}), bf16[32,7,2048]{2,1,0:T(8,128)(2,1)S(1)}, u32[]{:S(2)}, u32[]{:S(2)}) %all-to-all-start.1) | async-done | bytes 917536 | tf_op jit(solution)/shard_map/while/body/eval_jaxpr/all_to_all | solution.py:115
  422.3 13.1 %collective-permute-done = bf16[32,2048]{1,0:T(8,128)(2,1)S(1)} collective-permute-done((bf16[32,2048]{1,0:T(8,128)(2,1)S(1)}, bf16[32,2048]{1,0:T(8,128)(2,1)S(1)}, u32[]{:S(2)}, u32[]{:S(2)}) %collective-permute-start) | collective-permute-done | bytes 131104 | tf_op jit(solution)/shard_map/while/body/eval_jaxpr/ppermute | solution.py:22
  444.8 17.4 %all-to-all-done = bf16[32,7,2048]{2,1,0:T(8,128)(2,1)S(1)} async-done(((bf16[32,7,2048]{2,1,0:T(8,128)(2,1)}), bf16[32,7,2048]{2,1,0:T(8,128)(2,1)S(1)}, u32[]{:S(2)}, u32[]{:S(2)}) %all-to-all-start) | async-done | bytes 917536 | tf_op jit(solution)/shard_map/while/body/eval_jaxpr/all_to_all | solution.py:112
  462.3 8.9 conditional.3
  480.4 16.7 %all-to-all-done.1 = bf16[32,7,2048]{2,1,0:T(8,128)(2,1)S(1)} async-done(((bf16[32,7,2048]{2,1,0:T(8,128)(2,1)}), bf16[32,7,2048]{2,1,0:T(8,128)(2,1)S(1)}, u32[]{:S(2)}, u32[]{:S(2)}) %all-to-all-start.1) | async-done | bytes 917536 | tf_op jit(solution)/shard_map/while/body/eval_jaxpr/all_to_all | solution.py:115
  500.7 9.6 %collective-permute-done = bf16[32,2048]{1,0:T(8,128)(2,1)S(1)} collective-permute-done((bf16[32,2048]{1,0:T(8,128)(2,1)S(1)}, bf16[32,2048]{1,0:T(8,128)(2,1)S(1)}, u32[]{:S(2)}, u32[]{:S(2)}) %collective-permute-start) | collective-permute-done | bytes 131104 | tf_op jit(solution)/shard_map/while/body/eval_jaxpr/ppermute | solution.py:22
  522.1 17.8 %all-to-all-done = bf16[32,7,2048]{2,1,0:T(8,128)(2,1)S(1)} async-done(((bf16[32,7,2048]{2,1,0:T(8,128)(2,1)}), bf16[32,7,2048]{2,1,0:T(8,128)(2,1)S(1)}, u32[]{:S(2)}, u32[]{:S(2)}) %all-to-all-start) | async-done | bytes 917536 | tf_op jit(solution)/shard_map/while/body/eval_jaxpr/all_to_all | solution.py:112
  548.8 24.1 %all-to-all-done.1 = bf16[32,7,2048]{2,1,0:T(8,128)(2,1)S(1)} async-done(((bf16[32,7,2048]{2,1,0:T(8,128)(2,1)}), bf16[32,7,2048]{2,1,0:T(8,128)(2,1)S(1)}, u32[]{:S(2)}, u32[]{:S(2)}) %all-to-all-start.1) | async-done | bytes 917536 | tf_op jit(solution)/shard_map/while/body/eval_jaxpr/all_to_all | solution.py:115
  576.6 10.9 %collective-permute-done = bf16[32,2048]{1,0:T(8,128)(2,1)S(1)} collective-permute-done((bf16[32,2048]{1,0:T(8,128)(2,1)S(1)}, bf16[32,2048]{1,0:T(8,128)(2,1)S(1)}, u32[]{:S(2)}, u32[]{:S(2)}) %collective-permute-start) | collective-permute-done | bytes 131104 | tf_op jit(solution)/shard_map/while/body/eval_jaxpr/ppermute | solution.py:22
  591.0 8.3 all-to-all-start
  599.3 18.1 %all-to-all-done = bf16[32,7,2048]{2,1,0:T(8,128)(2,1)S(1)} async-done(((bf16[32,7,2048]{2,1,0:T(8,128)(2,1)}), bf16[32,7,2048]{2,1,0:T(8,128)(2,1)S(1)}, u32[]{:S(2)}, u32[]{:S(2)}) %all-to-all-start) | async-done | bytes 917536 | tf_op jit(solution)/shard_map/while/body/eval_jaxpr/all_to_all | solution.py:112
  618.8 8.4 all-to-all-start.1
  628.7 16.7 %all-to-all-done.1 = bf16[32,7,2048]{2,1,0:T(8,128)(2,1)S(1)} async-done(((bf16[32,7,2048]{2,1,0:T(8,128)(2,1)}), bf16[32,7,2048]{2,1,0:T(8,128)(2,1)S(1)}, u32[]{:S(2)}, u32[]{:S(2)}) %all-to-all-start.1) | async-done | bytes 917536 | tf_op jit(solution)/shard_map/while/body/eval_jaxpr/all_to_all | solution.py:115
  649.0 15.8 %collective-permute-done = bf16[32,2048]{1,0:T(8,128)(2,1)S(1)} collective-permute-done((bf16[32,2048]{1,0:T(8,128)(2,1)S(1)}, bf16[32,2048]{1,0:T(8,128)(2,1)S(1)}, u32[]{:S(2)}, u32[]{:S(2)}) %collective-permute-start) | collective-permute-done | bytes 131104 | tf_op jit(solution)/shard_map/while/body/eval_jaxpr/ppermute | solution.py:22
  668.2 8.3 all-to-all-start
  676.5 20.5 %all-to-all-done = bf16[32,7,2048]{2,1,0:T(8,128)(2,1)S(1)} async-done(((bf16[32,7,2048]{2,1,0:T(8,128)(2,1)}), bf16[32,7,2048]{2,1,0:T(8,128)(2,1)S(1)}, u32[]{:S(2)}, u32[]{:S(2)}) %all-to-all-start) | async-done | bytes 917536 | tf_op jit(solution)/shard_map/while/body/eval_jaxpr/all_to_all | solution.py:112
  698.4 10.2 %all-to-all-start.1 = ((bf16[32,7,2048]{2,1,0:T(8,128)(2,1)}), bf16[32,7,2048]{2,1,0:T(8,128)(2,1)S(1)}, u32[]{:S(2)}, u32[]{:S(2)}) async-start(bf16[32,7,2048]{2,1,0:T(8,128)(2,1)} %reshape.63), calls=%async_computation.1 | async-start | bytes 2097152 | tf_op jit(solution)/shard_map/while/body/eval_jaxpr/all_to_all | solution.py:115
  710.1 16.7 %all-to-all-done.1 = bf16[32,7,2048]{2,1,0:T(8,128)(2,1)S(1)} async-done(((bf16[32,7,2048]{2,1,0:T(8,128)(2,1)}), bf16[32,7,2048]{2,1,0:T(8,128)(2,1)S(1)}, u32[]{:S(2)}, u32[]{:S(2)}) %all-to-all-start.1) | async-done | bytes 917536 | tf_op jit(solution)/shard_map/while/body/eval_jaxpr/all_to_all | solution.py:115
  730.4 11.6 %collective-permute-done = bf16[32,2048]{1,0:T(8,128)(2,1)S(1)} collective-permute-done((bf16[32,2048]{1,0:T(8,128)(2,1)S(1)}, bf16[32,2048]{1,0:T(8,128)(2,1)S(1)}, u32[]{:S(2)}, u32[]{:S(2)}) %collective-permute-start) | collective-permute-done | bytes 131104 | tf_op jit(solution)/shard_map/while/body/eval_jaxpr/ppermute | solution.py:22
  745.4 8.3 all-to-all-start
  753.7 18.1 %all-to-all-done = bf16[32,7,2048]{2,1,0:T(8,128)(2,1)S(1)} async-done(((bf16[32,7,2048]{2,1,0:T(8,128)(2,1)}), bf16[32,7,2048]{2,1,0:T(8,128)(2,1)S(1)}, u32[]{:S(2)}, u32[]{:S(2)}) %all-to-all-start) | async-done | bytes 917536 | tf_op jit(solution)/shard_map/while/body/eval_jaxpr/all_to_all | solution.py:112
  782.9 16.7 %all-to-all-done.1 = bf16[32,7,2048]{2,1,0:T(8,128)(2,1)S(1)} async-done(((bf16[32,7,2048]{2,1,0:T(8,128)(2,1)}), bf16[32,7,2048]{2,1,0:T(8,128)(2,1)S(1)}, u32[]{:S(2)}, u32[]{:S(2)}) %all-to-all-start.1) | async-done | bytes 917536 | tf_op jit(solution)/shard_map/while/body/eval_jaxpr/all_to_all | solution.py:115
  803.2 16.0 %collective-permute-done = bf16[32,2048]{1,0:T(8,128)(2,1)S(1)} collective-permute-done((bf16[32,2048]{1,0:T(8,128)(2,1)S(1)}, bf16[32,2048]{1,0:T(8,128)(2,1)S(1)}, u32[]{:S(2)}, u32[]{:S(2)}) %collective-permute-start) | collective-permute-done | bytes 131104 | tf_op jit(solution)/shard_map/while/body/eval_jaxpr/ppermute | solution.py:22
  822.7 8.3 all-to-all-start
  831.0 20.9 %all-to-all-done = bf16[32,7,2048]{2,1,0:T(8,128)(2,1)S(1)} async-done(((bf16[32,7,2048]{2,1,0:T(8,128)(2,1)}), bf16[32,7,2048]{2,1,0:T(8,128)(2,1)S(1)}, u32[]{:S(2)}, u32[]{:S(2)}) %all-to-all-start) | async-done | bytes 917536 | tf_op jit(solution)/shard_map/while/body/eval_jaxpr/all_to_all | solution.py:112
  853.3 9.8 %all-to-all-start.1 = ((bf16[32,7,2048]{2,1,0:T(8,128)(2,1)}), bf16[32,7,2048]{2,1,0:T(8,128)(2,1)S(1)}, u32[]{:S(2)}, u32[]{:S(2)}) async-start(bf16[32,7,2048]{2,1,0:T(8,128)(2,1)} %reshape.63), calls=%async_computation.1 | async-start | bytes 2097152 | tf_op jit(solution)/shard_map/while/body/eval_jaxpr/all_to_all | solution.py:115
  864.6 16.7 %all-to-all-done.1 = bf16[32,7,2048]{2,1,0:T(8,128)(2,1)S(1)} async-done(((bf16[32,7,2048]{2,1,0:T(8,128)(2,1)}), bf16[32,7,2048]{2,1,0:T(8,128)(2,1)S(1)}, u32[]{:S(2)}, u32[]{:S(2)}) %all-to-all-start.1) | async-done | bytes 917536 | tf_op jit(solution)/shard_map/while/body/eval_jaxpr/all_to_all | solution.py:115
  884.9 11.6 %collective-permute-done = bf16[32,2048]{1,0:T(8,128)(2,1)S(1)} collective-permute-done((bf16[32,2048]{1,0:T(8,128)(2,1)S(1)}, bf16[32,2048]{1,0:T(8,128)(2,1)S(1)}, u32[]{:S(2)}, u32[]{:S(2)}) %collective-permute-start) | collective-permute-done | bytes 131104 | tf_op jit(solution)/shard_map/while/body/eval_jaxpr/ppermute | solution.py:22
  897.0 18.4 %all_to_all.29 = bf16[32,2,1024]{2,1,0:T(2,128)(2,1)S(1)} all-to-all(bf16[32,2,1024]{2,1,0:T(2,128)(2,1)S(1)} %reshape.60), channel_id=1, replica_groups=mesh['section'=8,'dp_0'=4,'dp_1'=8] {'dp_0','dp_1'}, dimensions={0} | all-to-all | bytes 262144 | tf_op jit(solution)/shard_map/all_to_all | solution.py:33
  (275 shorter events, 242.1 us)
Async XLA Ops:
  32.8 27.5 %all-to-all-start = ((bf16[32,7,2048]{2,1,0:T(8,128)(2,1)}), bf16[32,7,2048]{2,1,0:T(8,128)(2,1)S(1)}, u32[]{:S(2)}, u32[]{:S(2)}) async-start(bf16[32,7,2048]{2,1,0:T(8,128)(2,1)} %copy.69), calls=%async_computation | async-start | bytes 2097152 | tf_op jit(solution)/shard_map/while/body/eval_jaxpr/all_to_all | solution.py:112
  61.7 28.5 %all-to-all-start.1 = ((bf16[32,7,2048]{2,1,0:T(8,128)(2,1)}), bf16[32,7,2048]{2,1,0:T(8,128)(2,1)S(1)}, u32[]{:S(2)}, u32[]{:S(2)}) async-start(bf16[32,7,2048]{2,1,0:T(8,128)(2,1)} %reshape.63), calls=%async_computation.1 | async-start | bytes 2097152 | tf_op jit(solution)/shard_map/while/body/eval_jaxpr/all_to_all | solution.py:115
  91.6 6.3 collective-permute-start
  101.3 33.9 %all-to-all-start = ((bf16[32,7,2048]{2,1,0:T(8,128)(2,1)}), bf16[32,7,2048]{2,1,0:T(8,128)(2,1)S(1)}, u32[]{:S(2)}, u32[]{:S(2)}) async-start(bf16[32,7,2048]{2,1,0:T(8,128)(2,1)} %copy.69), calls=%async_computation | async-start | bytes 2097152 | tf_op jit(solution)/shard_map/while/body/eval_jaxpr/all_to_all | solution.py:112
  136.6 33.2 %all-to-all-start.1 = ((bf16[32,7,2048]{2,1,0:T(8,128)(2,1)}), bf16[32,7,2048]{2,1,0:T(8,128)(2,1)S(1)}, u32[]{:S(2)}, u32[]{:S(2)}) async-start(bf16[32,7,2048]{2,1,0:T(8,128)(2,1)} %reshape.63), calls=%async_computation.1 | async-start | bytes 2097152 | tf_op jit(solution)/shard_map/while/body/eval_jaxpr/all_to_all | solution.py:115
  171.2 10.3 %collective-permute-start = (bf16[32,2048]{1,0:T(8,128)(2,1)S(1)}, bf16[32,2048]{1,0:T(8,128)(2,1)S(1)}, u32[]{:S(2)}, u32[]{:S(2)}) collective-permute-start(bf16[32,2048]{1,0:T(8,128)(2,1)S(1)} %get-tuple-element.542), channel_id=1, source_target_pairs={{0,32},{32,64},{64,96},{96,128},{128,160},{160,192},{192,224},{1,3... | collective-permute-start | bytes 393224 | tf_op jit(solution)/shard_map/while/body/eval_jaxpr/ppermute | solution.py:22
  185.0 29.2 %all-to-all-start = ((bf16[32,7,2048]{2,1,0:T(8,128)(2,1)}), bf16[32,7,2048]{2,1,0:T(8,128)(2,1)S(1)}, u32[]{:S(2)}, u32[]{:S(2)}) async-start(bf16[32,7,2048]{2,1,0:T(8,128)(2,1)} %copy.69), calls=%async_computation | async-start | bytes 2097152 | tf_op jit(solution)/shard_map/while/body/eval_jaxpr/all_to_all | solution.py:112
  224.4 22.4 %all-to-all-start.1 = ((bf16[32,7,2048]{2,1,0:T(8,128)(2,1)}), bf16[32,7,2048]{2,1,0:T(8,128)(2,1)S(1)}, u32[]{:S(2)}, u32[]{:S(2)}) async-start(bf16[32,7,2048]{2,1,0:T(8,128)(2,1)} %reshape.63), calls=%async_computation.1 | async-start | bytes 2097152 | tf_op jit(solution)/shard_map/while/body/eval_jaxpr/all_to_all | solution.py:115
  248.2 19.9 %collective-permute-start = (bf16[32,2048]{1,0:T(8,128)(2,1)S(1)}, bf16[32,2048]{1,0:T(8,128)(2,1)S(1)}, u32[]{:S(2)}, u32[]{:S(2)}) collective-permute-start(bf16[32,2048]{1,0:T(8,128)(2,1)S(1)} %get-tuple-element.542), channel_id=1, source_target_pairs={{0,32},{32,64},{64,96},{96,128},{128,160},{160,192},{192,224},{1,3... | collective-permute-start | bytes 393224 | tf_op jit(solution)/shard_map/while/body/eval_jaxpr/ppermute | solution.py:22
  271.6 26.4 %all-to-all-start = ((bf16[32,7,2048]{2,1,0:T(8,128)(2,1)}), bf16[32,7,2048]{2,1,0:T(8,128)(2,1)S(1)}, u32[]{:S(2)}, u32[]{:S(2)}) async-start(bf16[32,7,2048]{2,1,0:T(8,128)(2,1)} %copy.69), calls=%async_computation | async-start | bytes 2097152 | tf_op jit(solution)/shard_map/while/body/eval_jaxpr/all_to_all | solution.py:112
  308.2 24.4 %all-to-all-start.1 = ((bf16[32,7,2048]{2,1,0:T(8,128)(2,1)}), bf16[32,7,2048]{2,1,0:T(8,128)(2,1)S(1)}, u32[]{:S(2)}, u32[]{:S(2)}) async-start(bf16[32,7,2048]{2,1,0:T(8,128)(2,1)} %reshape.63), calls=%async_computation.1 | async-start | bytes 2097152 | tf_op jit(solution)/shard_map/while/body/eval_jaxpr/all_to_all | solution.py:115
  334.0 20.2 %collective-permute-start = (bf16[32,2048]{1,0:T(8,128)(2,1)S(1)}, bf16[32,2048]{1,0:T(8,128)(2,1)S(1)}, u32[]{:S(2)}, u32[]{:S(2)}) collective-permute-start(bf16[32,2048]{1,0:T(8,128)(2,1)S(1)} %get-tuple-element.542), channel_id=1, source_target_pairs={{0,32},{32,64},{64,96},{96,128},{128,160},{160,192},{192,224},{1,3... | collective-permute-start | bytes 393224 | tf_op jit(solution)/shard_map/while/body/eval_jaxpr/ppermute | solution.py:22
  357.6 26.4 %all-to-all-start = ((bf16[32,7,2048]{2,1,0:T(8,128)(2,1)}), bf16[32,7,2048]{2,1,0:T(8,128)(2,1)S(1)}, u32[]{:S(2)}, u32[]{:S(2)}) async-start(bf16[32,7,2048]{2,1,0:T(8,128)(2,1)} %copy.69), calls=%async_computation | async-start | bytes 2097152 | tf_op jit(solution)/shard_map/while/body/eval_jaxpr/all_to_all | solution.py:112
  394.3 24.4 %all-to-all-start.1 = ((bf16[32,7,2048]{2,1,0:T(8,128)(2,1)}), bf16[32,7,2048]{2,1,0:T(8,128)(2,1)S(1)}, u32[]{:S(2)}, u32[]{:S(2)}) async-start(bf16[32,7,2048]{2,1,0:T(8,128)(2,1)} %reshape.63), calls=%async_computation.1 | async-start | bytes 2097152 | tf_op jit(solution)/shard_map/while/body/eval_jaxpr/all_to_all | solution.py:115
  420.0 15.4 %collective-permute-start = (bf16[32,2048]{1,0:T(8,128)(2,1)S(1)}, bf16[32,2048]{1,0:T(8,128)(2,1)S(1)}, u32[]{:S(2)}, u32[]{:S(2)}) collective-permute-start(bf16[32,2048]{1,0:T(8,128)(2,1)S(1)} %get-tuple-element.542), channel_id=1, source_target_pairs={{0,32},{32,64},{64,96},{96,128},{128,160},{160,192},{192,224},{1,3... | collective-permute-start | bytes 393224 | tf_op jit(solution)/shard_map/while/body/eval_jaxpr/ppermute | solution.py:22
  438.9 23.4 %all-to-all-start = ((bf16[32,7,2048]{2,1,0:T(8,128)(2,1)}), bf16[32,7,2048]{2,1,0:T(8,128)(2,1)S(1)}, u32[]{:S(2)}, u32[]{:S(2)}) async-start(bf16[32,7,2048]{2,1,0:T(8,128)(2,1)} %copy.69), calls=%async_computation | async-start | bytes 2097152 | tf_op jit(solution)/shard_map/while/body/eval_jaxpr/all_to_all | solution.py:112
  472.5 24.6 %all-to-all-start.1 = ((bf16[32,7,2048]{2,1,0:T(8,128)(2,1)}), bf16[32,7,2048]{2,1,0:T(8,128)(2,1)S(1)}, u32[]{:S(2)}, u32[]{:S(2)}) async-start(bf16[32,7,2048]{2,1,0:T(8,128)(2,1)} %reshape.63), calls=%async_computation.1 | async-start | bytes 2097152 | tf_op jit(solution)/shard_map/while/body/eval_jaxpr/all_to_all | solution.py:115
  498.5 11.8 %collective-permute-start = (bf16[32,2048]{1,0:T(8,128)(2,1)S(1)}, bf16[32,2048]{1,0:T(8,128)(2,1)S(1)}, u32[]{:S(2)}, u32[]{:S(2)}) collective-permute-start(bf16[32,2048]{1,0:T(8,128)(2,1)S(1)} %get-tuple-element.542), channel_id=1, source_target_pairs={{0,32},{32,64},{64,96},{96,128},{128,160},{160,192},{192,224},{1,3... | collective-permute-start | bytes 393224 | tf_op jit(solution)/shard_map/while/body/eval_jaxpr/ppermute | solution.py:22
  513.8 26.1 %all-to-all-start = ((bf16[32,7,2048]{2,1,0:T(8,128)(2,1)}), bf16[32,7,2048]{2,1,0:T(8,128)(2,1)S(1)}, u32[]{:S(2)}, u32[]{:S(2)}) async-start(bf16[32,7,2048]{2,1,0:T(8,128)(2,1)} %copy.69), calls=%async_computation | async-start | bytes 2097152 | tf_op jit(solution)/shard_map/while/body/eval_jaxpr/all_to_all | solution.py:112
  541.3 31.7 %all-to-all-start.1 = ((bf16[32,7,2048]{2,1,0:T(8,128)(2,1)}), bf16[32,7,2048]{2,1,0:T(8,128)(2,1)S(1)}, u32[]{:S(2)}, u32[]{:S(2)}) async-start(bf16[32,7,2048]{2,1,0:T(8,128)(2,1)} %reshape.63), calls=%async_computation.1 | async-start | bytes 2097152 | tf_op jit(solution)/shard_map/while/body/eval_jaxpr/all_to_all | solution.py:115
  574.4 13.2 %collective-permute-start = (bf16[32,2048]{1,0:T(8,128)(2,1)S(1)}, bf16[32,2048]{1,0:T(8,128)(2,1)S(1)}, u32[]{:S(2)}, u32[]{:S(2)}) collective-permute-start(bf16[32,2048]{1,0:T(8,128)(2,1)S(1)} %get-tuple-element.542), channel_id=1, source_target_pairs={{0,32},{32,64},{64,96},{96,128},{128,160},{160,192},{192,224},{1,3... | collective-permute-start | bytes 393224 | tf_op jit(solution)/shard_map/while/body/eval_jaxpr/ppermute | solution.py:22
  591.0 26.4 %all-to-all-start = ((bf16[32,7,2048]{2,1,0:T(8,128)(2,1)}), bf16[32,7,2048]{2,1,0:T(8,128)(2,1)S(1)}, u32[]{:S(2)}, u32[]{:S(2)}) async-start(bf16[32,7,2048]{2,1,0:T(8,128)(2,1)} %copy.69), calls=%async_computation | async-start | bytes 2097152 | tf_op jit(solution)/shard_map/while/body/eval_jaxpr/all_to_all | solution.py:112
  618.8 26.5 %all-to-all-start.1 = ((bf16[32,7,2048]{2,1,0:T(8,128)(2,1)}), bf16[32,7,2048]{2,1,0:T(8,128)(2,1)S(1)}, u32[]{:S(2)}, u32[]{:S(2)}) async-start(bf16[32,7,2048]{2,1,0:T(8,128)(2,1)} %reshape.63), calls=%async_computation.1 | async-start | bytes 2097152 | tf_op jit(solution)/shard_map/while/body/eval_jaxpr/all_to_all | solution.py:115
  646.7 18.0 %collective-permute-start = (bf16[32,2048]{1,0:T(8,128)(2,1)S(1)}, bf16[32,2048]{1,0:T(8,128)(2,1)S(1)}, u32[]{:S(2)}, u32[]{:S(2)}) collective-permute-start(bf16[32,2048]{1,0:T(8,128)(2,1)S(1)} %get-tuple-element.542), channel_id=1, source_target_pairs={{0,32},{32,64},{64,96},{96,128},{128,160},{160,192},{192,224},{1,3... | collective-permute-start | bytes 393224 | tf_op jit(solution)/shard_map/while/body/eval_jaxpr/ppermute | solution.py:22
  668.2 28.8 %all-to-all-start = ((bf16[32,7,2048]{2,1,0:T(8,128)(2,1)}), bf16[32,7,2048]{2,1,0:T(8,128)(2,1)S(1)}, u32[]{:S(2)}, u32[]{:S(2)}) async-start(bf16[32,7,2048]{2,1,0:T(8,128)(2,1)} %copy.69), calls=%async_computation | async-start | bytes 2097152 | tf_op jit(solution)/shard_map/while/body/eval_jaxpr/all_to_all | solution.py:112
  698.4 28.3 %all-to-all-start.1 = ((bf16[32,7,2048]{2,1,0:T(8,128)(2,1)}), bf16[32,7,2048]{2,1,0:T(8,128)(2,1)S(1)}, u32[]{:S(2)}, u32[]{:S(2)}) async-start(bf16[32,7,2048]{2,1,0:T(8,128)(2,1)} %reshape.63), calls=%async_computation.1 | async-start | bytes 2097152 | tf_op jit(solution)/shard_map/while/body/eval_jaxpr/all_to_all | solution.py:115
  728.2 13.8 %collective-permute-start = (bf16[32,2048]{1,0:T(8,128)(2,1)S(1)}, bf16[32,2048]{1,0:T(8,128)(2,1)S(1)}, u32[]{:S(2)}, u32[]{:S(2)}) collective-permute-start(bf16[32,2048]{1,0:T(8,128)(2,1)S(1)} %get-tuple-element.542), channel_id=1, source_target_pairs={{0,32},{32,64},{64,96},{96,128},{128,160},{160,192},{192,224},{1,3... | collective-permute-start | bytes 393224 | tf_op jit(solution)/shard_map/while/body/eval_jaxpr/ppermute | solution.py:22
  745.4 26.4 %all-to-all-start = ((bf16[32,7,2048]{2,1,0:T(8,128)(2,1)}), bf16[32,7,2048]{2,1,0:T(8,128)(2,1)S(1)}, u32[]{:S(2)}, u32[]{:S(2)}) async-start(bf16[32,7,2048]{2,1,0:T(8,128)(2,1)} %copy.69), calls=%async_computation | async-start | bytes 2097152 | tf_op jit(solution)/shard_map/while/body/eval_jaxpr/all_to_all | solution.py:112
  773.2 26.3 %all-to-all-start.1 = ((bf16[32,7,2048]{2,1,0:T(8,128)(2,1)}), bf16[32,7,2048]{2,1,0:T(8,128)(2,1)S(1)}, u32[]{:S(2)}, u32[]{:S(2)}) async-start(bf16[32,7,2048]{2,1,0:T(8,128)(2,1)} %reshape.63), calls=%async_computation.1 | async-start | bytes 2097152 | tf_op jit(solution)/shard_map/while/body/eval_jaxpr/all_to_all | solution.py:115
  801.0 18.2 %collective-permute-start = (bf16[32,2048]{1,0:T(8,128)(2,1)S(1)}, bf16[32,2048]{1,0:T(8,128)(2,1)S(1)}, u32[]{:S(2)}, u32[]{:S(2)}) collective-permute-start(bf16[32,2048]{1,0:T(8,128)(2,1)S(1)} %get-tuple-element.542), channel_id=1, source_target_pairs={{0,32},{32,64},{64,96},{96,128},{128,160},{160,192},{192,224},{1,3... | collective-permute-start | bytes 393224 | tf_op jit(solution)/shard_map/while/body/eval_jaxpr/ppermute | solution.py:22
  822.7 29.2 %all-to-all-start = ((bf16[32,7,2048]{2,1,0:T(8,128)(2,1)}), bf16[32,7,2048]{2,1,0:T(8,128)(2,1)S(1)}, u32[]{:S(2)}, u32[]{:S(2)}) async-start(bf16[32,7,2048]{2,1,0:T(8,128)(2,1)} %copy.69), calls=%async_computation | async-start | bytes 2097152 | tf_op jit(solution)/shard_map/while/body/eval_jaxpr/all_to_all | solution.py:112
  853.3 27.9 %all-to-all-start.1 = ((bf16[32,7,2048]{2,1,0:T(8,128)(2,1)}), bf16[32,7,2048]{2,1,0:T(8,128)(2,1)S(1)}, u32[]{:S(2)}, u32[]{:S(2)}) async-start(bf16[32,7,2048]{2,1,0:T(8,128)(2,1)} %reshape.63), calls=%async_computation.1 | async-start | bytes 2097152 | tf_op jit(solution)/shard_map/while/body/eval_jaxpr/all_to_all | solution.py:115
  882.6 13.8 %collective-permute-start = (bf16[32,2048]{1,0:T(8,128)(2,1)S(1)}, bf16[32,2048]{1,0:T(8,128)(2,1)S(1)}, u32[]{:S(2)}, u32[]{:S(2)}) collective-permute-start(bf16[32,2048]{1,0:T(8,128)(2,1)S(1)} %get-tuple-element.542), channel_id=1, source_target_pairs={{0,32},{32,64},{64,96},{96,128},{128,160},{160,192},{192,224},{1,3... | collective-permute-start | bytes 393224 | tf_op jit(solution)/shard_map/while/body/eval_jaxpr/ppermute | solution.py:22

commit v2 on v0

v2 whole, which is shorter than its diff:
```python
import functools

import jax
import jax.numpy as jnp
from jax import lax
from jax.experimental import pallas as pl
from jax.experimental.pallas import tpu as pltpu
from jax.sharding import Mesh
from jax.sharding import PartitionSpec as P

EPSILON = 1e-06
MESH = pl.DeviceIdType.MESH
BF16 = jnp.bfloat16
F32 = jnp.float32
CAP = 7
PARTS = 8
GROUP = CAP * PARTS
TILES = GROUP // 8


def dot(a, b):
    return jnp.dot(a, b, preferred_element_type=F32)


def dot_nt(a, b):
    return lax.dot_general(a, b, (((1,), (1,)), ((), ())), preferred_element_type=F32)


def dot_tn(a, b):
    return lax.dot_general(a, b, (((0,), (0,)), ((), ())), preferred_element_type=F32)


def remote(src, dst, send_sem, recv_sem, device):
    return pltpu.make_async_remote_copy(
        src_ref=src, dst_ref=dst, send_sem=send_sem, recv_sem=recv_sem, device_id=device, device_id_type=MESH
    )


def batches_of(nx, nz):
    pairs = [[nz // 2, 0]] + [[d, nz - d] for d in range(nz // 2 - 1, 0, -1)]
    pairs = pairs[:-2] + [pairs[-2] + pairs[-1]]
    steps = sorted(range(nx), key=lambda i: (-min(i, nx - i), i))
    return [[(k, i) for k in ks for i in steps] for ks in pairs], [k for ks in pairs for k in ks], steps


def kernel(
    sizes,
    tokens_hbm,
    gain_hbm,
    router_hbm,
    routing_hbm,
    gate_hbm,
    up_hbm,
    down_hbm,
    out,
    grad,
    w_gate,
    w_up,
    w_down,
    w_router,
    gain,
    routing,
    states,
    states_before,
    normed_all,
    slope_all,
    code_all,
    match_all,
    pattern,
    pattern_t,
    spread,
    sent,
    arrived,
    hidden,
    regroup,
    regroup_t,
    whole,
    paired,
    produced,
    returned,
    combine,
    naming,
    naming_before,
    count_own,
    count_in,
    grad_own,
    grad_in,
    w_sem,
    in_sem,
    d_send,
    d_recv,
    r_send,
    r_recv,
    own_sem,
    own_send,
    side_send,
    side_recv,
    o_send,
    o_recv,
    c_send,
    c_recv,
    g_send,
    g_recv,
    go,
):
    sections, nx, nz, total_rows = sizes
    micro, stacked, part_width = out.shape
    rows, width = stacked // PARTS, part_width * PARTS
    experts = w_router.shape[0]
    topk = routing.shape[0]
    replicas = nx * nz
    slots = replicas * GROUP
    s = lax.axis_index("section")
    x = lax.axis_index("dp_0")
    z = lax.axis_index("dp_1")
    batches, k_order, i_order = batches_of(nx, nz)
    order = [step for batch in batches for step in batch]
    own = order.index((0, 0))
    starts = [0]
    for batch in batches:
        starts.append(starts[-1] + len(batch))
    own_batch = max(b for b in range(len(batches)) if starts[b] <= own)
    last = s == sections - 1
    quad_rows = nx * 8

    def ahead(j):
        k, i = order[j]
        return {"dp_0": lax.rem(x + i, nx), "dp_1": lax.rem(z + k, nz)}

    def behind(j, section):
        k, i = order[j]
        return {"section": section, "dp_0": lax.rem(x + nx - i, nx), "dp_1": lax.rem(z + nz - k, nz)}

    others = [j for j in range(replicas) if j != own]

    small = [
        pltpu.make_async_copy(routing_hbm, routing, in_sem.at[0]),
        pltpu.make_async_copy(gain_hbm, gain, in_sem.at[1]),
        pltpu.make_async_copy(router_hbm, w_router, in_sem.at[2]),
    ]
    for copy in small:
        copy.start()
    load_tokens = [
        pltpu.make_async_copy(
            tokens_hbm.at[:, :, pl.ds(p * part_width, part_width)], states.at[:, pl.ds(p * rows, rows)], in_sem.at[3 + p]
        )
        for p in range(PARTS)
    ]

    @pl.when(s == 0)
    def _():
        for copy in load_tokens:
            copy.start()

    weights = [
        pltpu.make_async_copy(gate_hbm, w_gate, w_sem.at[0]),
        pltpu.make_async_copy(up_hbm, w_up, w_sem.at[1]),
        pltpu.make_async_copy(down_hbm, w_down, w_sem.at[2]),
    ]
    for copy in weights:
        copy.start()

    barrier = pltpu.get_barrier_semaphore()
    for j in others:
        pl.semaphore_signal(barrier, inc=1, device_id=ahead(j), device_id_type=MESH)

    @pl.when(s > 0)
    def _():
        for j in range(replicas):
            pl.semaphore_signal(barrier, inc=1, device_id=behind(j, s - 1), device_id_type=MESH)

    @pl.when(s < sections - 1)
    def _():
        pl.semaphore_signal(barrier, inc=1, device_id={"section": s + 1}, device_id_type=MESH)

    e_row = lax.broadcasted_iota(jnp.int32, (experts, rows), 0)
    before = (
        lax.broadcasted_iota(jnp.int32, (rows, rows), 0) < lax.broadcasted_iota(jnp.int32, (rows, rows), 1)
    ).astype(BF16)
    row = lax.broadcasted_iota(jnp.int32, (slots, experts), 0)
    k_pos = row // (GROUP * nx)
    i_pos = (row // GROUP) % nx
    k_of = jnp.zeros_like(row)
    for p, k in enumerate(k_order):
        k_of = jnp.where(k_pos == p, k, k_of)
    i_of = jnp.zeros_like(row)
    for p, i in enumerate(i_order):
        i_of = jnp.where(i_pos == p, i, i_of)
    zz = k_of + z
    zz = jnp.where(zz >= nz, zz - nz, zz)
    xx = i_of + x
    xx = jnp.where(xx >= nx, xx - nx, xx)
    spread[...] = (lax.broadcasted_iota(jnp.int32, (slots, experts), 1) == xx * nz + zz).astype(BF16)

    g_place = lax.broadcasted_iota(jnp.int32, (slots, stacked), 0) % GROUP
    g_part = lax.broadcasted_iota(jnp.int32, (slots, stacked), 1) // rows
    pattern[...] = jnp.where(g_place // CAP == g_part, g_place % CAP, -9).astype(F32)
    t_place = lax.broadcasted_iota(jnp.int32, (stacked, slots), 1) % GROUP
    t_part = lax.broadcasted_iota(jnp.int32, (stacked, slots), 0) // rows
    pattern_t[...] = jnp.where(t_place // CAP == t_part, t_place % CAP, -9).astype(F32)

    def regrouping(shape, tall, wide):
        there = lax.broadcasted_iota(jnp.int32, shape, tall)
        here = lax.broadcasted_iota(jnp.int32, shape, wide)
        inside = here % GROUP
        same = jnp.logical_and(there // quad_rows == inside // CAP, (there % quad_rows) // 8 == here // GROUP)
        return jnp.logical_and(same, there % 8 == inside % CAP).astype(BF16)

    regroup[...] = regrouping(regroup.shape, 0, 1)
    regroup_t[...] = regrouping(regroup_t.shape, 1, 0)
    count_own[...] = jnp.zeros_like(count_own)

    def stack(block):
        return jnp.concatenate([block] * PARTS, axis=0)

    def prepare(m, _):
        hot = jnp.zeros((experts, rows), F32)
        for k in range(topk):
            hot = hot + (routing[k, pl.ds(m, 1)] == e_row).astype(F32)
        rank = dot(hot.astype(BF16), before)
        code = jnp.where(hot > 0, rank, -1.0).T
        count_own[...] = count_own[...] + jnp.sum((code >= 0).astype(F32), axis=0, keepdims=True)
        code_all[m] = code
        there = dot_nt(spread[...], stack(code.astype(BF16)))
        match_all[m] = (there == pattern[...]).astype(BF16)
        return 0

    def combining(code, mixing):
        there = dot_nt(stack(code), spread[...])
        share_there = dot_nt(stack(mixing), spread[...])
        return jnp.where(there == pattern_t[...], share_there, 0.0).astype(BF16)

    for copy in small:
        copy.wait()
    prepare(0, 0)

    @pl.when(s > 0)
    def _():
        lax.fori_loop(1, micro, prepare, 0)

    @pl.when(s == 0)
    def _():
        for copy in load_tokens:
            copy.wait()

    upward = (s < sections - 1).astype(jnp.int32)
    downward = (s > 0).astype(jnp.int32)
    pl.semaphore_wait(barrier, (replicas - 1) + replicas * upward + downward)

    count_copies = [remote(count_own, count_in.at[j], c_send, c_recv, ahead(j)) for j in others]

    def quad(q):
        return pl.ds(q * nx * GROUP, nx * GROUP)

    def span(b):
        return pl.ds(starts[b] * GROUP, (starts[b + 1] - starts[b]) * GROUP)

    def bytes_of(b, whole=True):
        count = starts[b + 1] - starts[b] - (1 if b == own_batch and not whole else 0)
        return pl.ds(starts[b] * TILES, count * TILES)

    def at(j):
        return pl.ds(j * TILES, TILES)

    def wait_sent(ref, b, sem):
        part = ref.at[bytes_of(b, False)]
        remote(part, part, sem.at[b], d_recv.at[0, b], ahead(0)).wait_send()

    def wait_back(index, b):
        part = returned.at[index, bytes_of(b)]
        remote(part, part, r_send.at[b], r_recv.at[index, b], ahead(0)).wait_recv()

    def keep(m):
        return pltpu.make_async_copy(sent.at[at(own)], arrived.at[m, at(own)], own_sem)

    def back(j, b, index, section, send_sem):
        return remote(produced.at[at(j)], returned.at[index, at(j)], send_sem, r_recv.at[index, b], behind(j, section))

    def side(m, section):
        here = {"section": section}
        return [
            remote(states.at[m], states_before.at[m], side_send.at[0, m], side_recv.at[0, m], here),
            remote(naming.at[m], naming_before.at[m], side_send.at[1, m], side_recv.at[1, m], here),
        ]

    def give(m, section):
        return remote(states.at[m], out.at[m], o_send.at[m], o_recv.at[m], {"section": section})

    def expert_ffn(m, b):
        quads = (starts[b + 1] - starts[b]) // nx
        count = quads * quad_rows
        received = arrived.at[m].reshape(slots, part_width)
        for q in range(quads):
            mine = dot(regroup[...], received[quad(starts[b] // nx + q)]).astype(BF16)
            for p in range(PARTS):
                whole[pl.ds(q * quad_rows, quad_rows), p * part_width : (p + 1) * part_width] = mine[
                    p * quad_rows : (p + 1) * quad_rows
                ]
        used = pl.ds(0, count)
        here = whole[used]
        piece = 256

        def inner(t, _):
            cols = pl.ds(pl.multiple_of(t * piece, piece), piece)
            gated = dot(here, w_gate[:, cols])
            upward = dot(here, w_up[:, cols])
            hidden[used, cols] = (gated / (1.0 + jnp.exp(-gated)) * upward).astype(BF16)
            return 0

        lax.fori_loop(0, w_gate.shape[1] // piece, inner, 0)
        now = hidden[used]

        def outer(t, _):
            cols = pl.ds(pl.multiple_of(t * 2 * part_width, 2 * part_width), 2 * part_width)
            made = dot(now, w_down[:, cols]).astype(BF16)
            for h in range(2):
                at_row = pl.multiple_of((2 * t + h) * quad_rows, quad_rows)
                for q in range(quads):
                    paired[q, pl.ds(at_row, quad_rows)] = made[
                        q * quad_rows : (q + 1) * quad_rows, h * part_width : (h + 1) * part_width
                    ]
            return 0

        lax.fori_loop(0, PARTS // 2, outer, 0)
        sending = produced.reshape(slots, part_width)
        for q in range(quads):
            sending[quad(starts[b] // nx + q)] = dot(regroup_t[...], paired[q]).astype(BF16)

    def mixed_rows(matrix, index):
        total = None
        for b in range(len(batches)):
            wait_back(index, b)
            first, past = starts[b] * GROUP, starts[b + 1] * GROUP
            part = dot(matrix[:, first:past], returned.at[index].reshape(slots, part_width)[span(b)])
            total = part if total is None else total + part
        return total

    def one(m, _):
        @pl.when(s > 0)
        def _():
            for copy in side(m, s):
                copy.wait_recv()
            combine[...] = combining(naming_before[m, 0], naming_before[m, 1])
            states[m] = (states_before[m].astype(F32) + mixed_rows(combine, m)).astype(BF16)
            give(m, s - 1).start()

        @pl.when(jnp.logical_and(s == 0, m > 0))
        def _():
            pl.semaphore_wait(go, 1)

        values = states[m].astype(F32)
        squares = jnp.sum(values * values, axis=-1, keepdims=True)
        scale = lax.rsqrt(sum(squares[p * rows : (p + 1) * rows] for p in range(PARTS)) / width + EPSILON)
        for p in range(PARTS):
            factor = gain[:, p * part_width : (p + 1) * part_width].astype(F32)
            here = slice(p * rows, (p + 1) * rows)
            normed_all[m, here] = (values[here] * scale * factor).astype(BF16)
        normed = normed_all[m]

        for b in range(len(batches)):
            @pl.when(m > 0)
            def _():
                wait_sent(sent, b, d_send)

            sent.reshape(slots, part_width)[span(b)] = dot(match_all[m, span(b)], normed).astype(BF16)
            for j in range(starts[b], starts[b + 1]):
                if j != own:
                    remote(sent.at[at(j)], arrived.at[m, at(j)], d_send.at[b], d_recv.at[m, b], ahead(j)).start()
                else:
                    keep(m).start()

        logits = sum(
            dot_nt(normed[p * rows : (p + 1) * rows], w_router[:, p * part_width : (p + 1) * part_width])
            for p in range(PARTS)
        )
        exps = jnp.exp(logits)
        probs = exps / jnp.sum(exps, axis=-1, keepdims=True)
        chosen = jnp.where(code_all[m] >= 0, probs, 0.0)
        mixing = (chosen / jnp.sum(chosen, axis=-1, keepdims=True)).astype(BF16)
        naming[m, 0] = code_all[m].astype(BF16)
        naming[m, 1] = mixing
        slope_all[m] = probs

        @pl.when(s < sections - 1)
        def _():
            for copy in side(m, s + 1):
                copy.start()

        @pl.when(jnp.logical_and(m == 0, s == 0))
        def _():
            lax.fori_loop(1, micro, prepare, 0)

        @pl.when(m == 0)
        def _():
            for copy in count_copies:
                copy.start()
            count_in[own] = count_own[...]
            for copy in weights:
                copy.wait()

        keep(m).wait()
        for b in range(len(batches)):
            part = arrived.at[m, bytes_of(b, False)]
            remote(part, part, d_send.at[b], d_recv.at[m, b], ahead(0)).wait_recv()

            expert_ffn(m, b)
            index = jnp.where(last, micro + m, m)
            to = jnp.where(last, s, s + 1)
            for j in range(starts[b], starts[b + 1]):
                if j != own:
                    back(j, b, index, to, r_send.at[b]).start()
                else:
                    @pl.when(jnp.logical_not(last))
                    def _():
                        back(j, b, m, s + 1, own_send).start()

                    @pl.when(last)
                    def _():
                        pltpu.make_async_copy(
                            produced.at[at(j)], returned.at[micro + m, at(j)], r_recv.at[micro + m, b]
                        ).start()

        @pl.when(m == micro - 1)
        def _():
            part = count_in.at[pl.ds(0, replicas - 1)]
            remote(part, part, c_send, c_recv, ahead(0)).wait()
            total = jnp.sum(count_in[...], axis=0)[0:1]
            share = experts * total / (topk * total_rows)
            for mm in range(micro):
                p = slope_all[mm]
                slope_all[mm] = p * (share - jnp.sum(p * share, axis=-1, keepdims=True))
            slope = slope_all[...].reshape(micro * rows, experts)
            high = slope.astype(BF16)
            low = (slope - high.astype(F32)).astype(BF16)
            for t in range(width // 128):
                h, c = divmod(t * 128, part_width)
                some = normed_all[:, h * rows : (h + 1) * rows, c : c + 128].reshape(micro * rows, 128)
                grad_own[t] = (dot_tn(high, some) + dot_tn(low, some)).astype(BF16)
            for j in others:
                k, i = order[j]
                where = lax.rem(x + i, nx) * nz + lax.rem(z + k, nz)
                remote(grad_own.at[where // 2], grad_in.at[j], g_send, g_recv, ahead(j)).start()
            grad_in[own] = grad_own[(x * nz + z) // 2]

        @pl.when(last)
        def _():
            combine[...] = combining(naming[m, 0], naming[m, 1])
            out[m] = (states[m].astype(F32) + mixed_rows(combine, micro + m)).astype(BF16)

        for b in range(len(batches)):
            wait_sent(produced, b, r_send)

        @pl.when(jnp.logical_not(last))
        def _():
            back(own, own_batch, m, s + 1, own_send).wait_send()

        @pl.when(jnp.logical_and(s == 1, m < micro - 1))
        def _():
            pl.semaphore_signal(go, inc=1, device_id={"section": 0}, device_id_type=MESH)

        return 0

    lax.fori_loop(0, micro, one, 0)

    part = grad_in.at[pl.ds(0, replicas - 1)]
    remote(part, part, g_send, g_recv, ahead(0)).wait()
    summed = jnp.sum(grad_in[...].astype(F32), axis=0)
    take = summed.shape[1] // 2
    grad[...] = jnp.where(lax.rem(z, 2) == 0, summed[:, :take], summed[:, take:])
    for b in range(len(batches)):
        wait_sent(sent, b, d_send)

    @pl.when(jnp.logical_not(last))
    def _():
        for m in range(micro):
            for copy in side(m, s + 1):
                copy.wait_send()
            give(m, s).wait_recv()

    @pl.when(s > 0)
    def _():
        for m in range(micro):
            give(m, s - 1).wait_send()


def on_device(sizes, tokens, norm_gain, router_weight, gate_weight, up_weight, down_weight, routing):
    sections, nx, nz, total_rows = sizes
    replicas = nx * nz
    micro, rows, width = tokens.shape
    experts = router_weight.shape[2]
    hidden = gate_weight.shape[3]
    topk = routing.shape[3]
    slots = replicas * GROUP
    part, stacked = width // PARTS, rows * PARTS
    quad = nx * 8
    most = 4 * quad
    vmem = pl.BlockSpec(memory_space=pltpu.VMEM)
    hbm = pl.BlockSpec(memory_space=pltpu.MemorySpace.HBM)
    dma = pltpu.SemaphoreType.DMA
    outputs, gradient = pl.pallas_call(
        functools.partial(kernel, sizes),
        out_shape=(
            jax.ShapeDtypeStruct((micro, stacked, part), BF16),
            jax.ShapeDtypeStruct((experts, width // replicas), F32),
        ),
        in_specs=[hbm] * 7,
        out_specs=(vmem, vmem),
        scratch_shapes=[
            pltpu.VMEM((width, hidden), BF16),
            pltpu.VMEM((width, hidden), BF16),
            pltpu.VMEM((hidden, width), BF16),
            pltpu.VMEM((experts, width), BF16),
            pltpu.VMEM((1, width), BF16),
            pltpu.VMEM((topk, micro, rows), jnp.int32),
            pltpu.VMEM((micro, stacked, part), BF16),
            pltpu.VMEM((micro, stacked, part), BF16),
            pltpu.VMEM((micro, stacked, part), BF16),
            pltpu.VMEM((micro, rows, experts), F32),
            pltpu.VMEM((micro, rows, experts), F32),
            pltpu.VMEM((micro, slots, stacked), BF16),
            pltpu.VMEM((slots, stacked), F32),
            pltpu.VMEM((stacked, slots), F32),
            pltpu.VMEM((slots, experts), BF16),
            pltpu.VMEM((slots // 8, 8, part), BF16),
            pltpu.VMEM((micro, slots // 8, 8, part), BF16),
            pltpu.VMEM((most, hidden), BF16),
            pltpu.VMEM((PARTS * quad, nx * GROUP), BF16),
            pltpu.VMEM((nx * GROUP, PARTS * quad), BF16),
            pltpu.VMEM((most, width), BF16),
            pltpu.VMEM((4, PARTS * quad, part), BF16),
            pltpu.VMEM((slots // 8, 8, part), BF16),
            pltpu.VMEM((2 * micro, slots // 8, 8, part), BF16),
            pltpu.VMEM((stacked, slots), BF16),
            pltpu.VMEM((micro, 2, rows, experts), BF16),
            pltpu.VMEM((micro, 2, rows, experts), BF16),
            pltpu.VMEM((8, experts), F32),
            pltpu.VMEM((replicas, 8, experts), F32),
            pltpu.VMEM((width // 128, experts, 128), BF16),
            pltpu.VMEM((replicas, experts, 128), BF16),
            dma((3,)),
            dma((3 + PARTS,)),
            dma((nz // 2,)),
            dma((micro, nz // 2)),
            dma((nz // 2,)),
            dma((2 * micro, nz // 2)),
            dma(()),
            dma(()),
            dma((2, micro)),
            dma((2, micro)),
            dma((micro,)),
            dma((micro,)),
            dma(()),
            dma(()),
            dma(()),
            dma(()),
            pltpu.SemaphoreType.REGULAR,
        ],
        compiler_params=pltpu.CompilerParams(
            collective_id=0, has_side_effects=True, vmem_limit_bytes=58 * 1024 * 1024
        ),
    )(tokens, norm_gain, router_weight[0].T, routing[0].transpose(2, 0, 1), gate_weight[0, 0], up_weight[0, 0], down_weight[0, 0])
    outputs = outputs.reshape(micro, PARTS, rows, part).transpose(0, 2, 1, 3).reshape(micro, rows, width)
    return outputs[None], gradient.T[None]


def solution(mesh):
    nx, nz = 4, mesh.shape["dp"] // 4
    torus = Mesh(mesh.devices.reshape(mesh.shape["section"], nx, nz), ("section", "dp_0", "dp_1"))
    dp = ("dp_0", "dp_1")

    def run(tokens, norm_gain, router_weight, gate_weight, up_weight, down_weight, routing):
        total_rows = tokens.shape[0] * tokens.shape[1]
        sizes = (mesh.shape["section"], nx, nz, total_rows)
        return jax.shard_map(
            functools.partial(on_device, sizes),
            mesh=torus,
            in_specs=(
                P(None, dp, None),
                P("section", None),
                P("section", None, None),
                P("section", dp, None, None),
                P("section", dp, None, None),
                P("section", dp, None, None),
                P("section", None, dp, None),
            ),
            out_specs=(P("section", None, dp, None), P("section", dp, None)),
            check_vma=False,
        )(tokens, norm_gain, router_weight, gate_weight, up_weight, down_weight, routing)

    return run
```

time: 920 us -> 381 us (0.41)
  the two profiles are of different devices: /device:TPU:8 before, /device:TPU:25 now
where the time goes in v2:
time: 381 us; the launch traced here: 380 us
  Pallas kernels  376 us (99%)
    pallas_call x1, Pallas kernels, on_device(): pl.pallas_call(functools.partial(kernel, sizes), out_shape=(jax.ShapeDtyp...  376 us

profile of v2, /device:TPU:25, one launch (start us, length us, event | category | flops | bytes accessed | tf_op | source)
XLA Modules:
  0.0 380.4 jit_solution(13262386297468136391)
XLA Ops:
  0.6 376.0 %shard_map.86 = (bf16[4,256,256]{2,1,0:T(8,128)(2,1)}, f32[32,64]{1,0:T(8,128)}) custom-call(bf16[4,32,2048]{2,1,0:T(8,128)(2,1)} %tokens_hbm.1, bf16[1,2048]{1,0:T(2,128)(2,1)} %gain_hbm.1, bf16[32,2048]{1,0:T(8,128)(2,1)} %bitcast.21, s32[6,4,32]{2,1,0:T(4,128)} %bitcast.23, bf16[2048,768]{1,0:T(8,128)(2,1)} %bitcast.17, bf16[2048,768]{1,0:T(8,128)(2,1)} %bitcast.18, ...), custom_call_target="tpu_custom_call" | custom-call | tf_op jit(solution)/shard_map/pallas_call | solution.py:500
  376.7 1.3 copy.9
  378.0 1.0 broadcast_in_dim_reshape.3
  379.0 1.3 copy.11

commit v3 on v2

--- a/solution.py
+++ b/solution.py
@@ -38,7 +38,6 @@
 
 def batches_of(nx, nz):
     pairs = [[nz // 2, 0]] + [[d, nz - d] for d in range(nz // 2 - 1, 0, -1)]
-    pairs = pairs[:-2] + [pairs[-2] + pairs[-1]]
     steps = sorted(range(nx), key=lambda i: (-min(i, nx - i), i))
     return [[(k, i) for k in ks for i in steps] for ks in pairs], [k for ks in pairs for k in ks], steps
 
@@ -104,8 +103,9 @@
     go,
 ):
     sections, nx, nz, total_rows = sizes
-    micro, stacked, part_width = out.shape
-    rows, width = stacked // PARTS, part_width * PARTS
+    micro, rows, width = out.shape
+    part_width = width // PARTS
+    stacked = rows * PARTS
     experts = w_router.shape[0]
     topk = routing.shape[0]
     replicas = nx * nz
@@ -177,9 +177,9 @@
     before = (
         lax.broadcasted_iota(jnp.int32, (rows, rows), 0) < lax.broadcasted_iota(jnp.int32, (rows, rows), 1)
     ).astype(BF16)
-    row = lax.broadcasted_iota(jnp.int32, (slots, experts), 0)
-    k_pos = row // (GROUP * nx)
-    i_pos = (row // GROUP) % nx
+    row = lax.broadcasted_iota(jnp.int32, (replicas, experts), 0)
+    k_pos = row // nx
+    i_pos = row % nx
     k_of = jnp.zeros_like(row)
     for p, k in enumerate(k_order):
         k_of = jnp.where(k_pos == p, k, k_of)
@@ -190,13 +190,15 @@
     zz = jnp.where(zz >= nz, zz - nz, zz)
     xx = i_of + x
     xx = jnp.where(xx >= nx, xx - nx, xx)
-    spread[...] = (lax.broadcasted_iota(jnp.int32, (slots, experts), 1) == xx * nz + zz).astype(BF16)
-
-    g_place = lax.broadcasted_iota(jnp.int32, (slots, stacked), 0) % GROUP
-    g_part = lax.broadcasted_iota(jnp.int32, (slots, stacked), 1) // rows
+    named = (lax.broadcasted_iota(jnp.int32, (replicas, experts), 1) == xx * nz + zz).astype(F32)
+    for j in range(replicas):
+        spread[pl.ds(j * GROUP, GROUP)] = jnp.broadcast_to(named[j : j + 1], (GROUP, experts)).astype(BF16)
+
+    g_place = lax.broadcasted_iota(jnp.int32, (GROUP, stacked), 0)
+    g_part = lax.broadcasted_iota(jnp.int32, (GROUP, stacked), 1) // rows
     pattern[...] = jnp.where(g_place // CAP == g_part, g_place % CAP, -9).astype(F32)
-    t_place = lax.broadcasted_iota(jnp.int32, (stacked, slots), 1) % GROUP
-    t_part = lax.broadcasted_iota(jnp.int32, (stacked, slots), 0) // rows
+    t_place = lax.broadcasted_iota(jnp.int32, (PARTS, slots), 1) % GROUP
+    t_part = lax.broadcasted_iota(jnp.int32, (PARTS, slots), 0)
     pattern_t[...] = jnp.where(t_place // CAP == t_part, t_place % CAP, -9).astype(F32)
 
     def regrouping(shape, tall, wide):
@@ -206,8 +208,6 @@
         same = jnp.logical_and(there // quad_rows == inside // CAP, (there % quad_rows) // 8 == here // GROUP)
         return jnp.logical_and(same, there % 8 == inside % CAP).astype(BF16)
 
-    regroup[...] = regrouping(regroup.shape, 0, 1)
-    regroup_t[...] = regrouping(regroup_t.shape, 1, 0)
     count_own[...] = jnp.zeros_like(count_own)
 
     def stack(block):
@@ -222,21 +222,31 @@
         count_own[...] = count_own[...] + jnp.sum((code >= 0).astype(F32), axis=0, keepdims=True)
         code_all[m] = code
         there = dot_nt(spread[...], stack(code.astype(BF16)))
-        match_all[m] = (there == pattern[...]).astype(BF16)
+        for j in range(replicas):
+            group = slice(j * GROUP, (j + 1) * GROUP)
+            match_all[m, group] = (there[group] == pattern[...]).astype(BF16)
         return 0
 
     def combining(code, mixing):
         there = dot_nt(stack(code), spread[...])
         share_there = dot_nt(stack(mixing), spread[...])
-        return jnp.where(there == pattern_t[...], share_there, 0.0).astype(BF16)
+        for p in range(PARTS):
+            here = slice(p * rows, (p + 1) * rows)
+            fits = there[here] == pattern_t[p : p + 1]
+            combine[here] = jnp.where(fits, share_there[here], 0.0).astype(BF16)
 
     for copy in small:
         copy.wait()
     prepare(0, 0)
 
+    def prepare_rest():
+        regroup[...] = regrouping(regroup.shape, 0, 1)
+        regroup_t[...] = regrouping(regroup_t.shape, 1, 0)
+        lax.fori_loop(1, micro, prepare, 0)
+
     @pl.when(s > 0)
     def _():
-        lax.fori_loop(1, micro, prepare, 0)
+        prepare_rest()
 
     @pl.when(s == 0)
     def _():
@@ -284,7 +294,16 @@
         ]
 
     def give(m, section):
-        return remote(states.at[m], out.at[m], o_send.at[m], o_recv.at[m], {"section": section})
+        return [
+            remote(
+                states.at[m, pl.ds(p * rows, rows)],
+                out.at[m, :, pl.ds(p * part_width, part_width)],
+                o_send.at[m],
+                o_recv.at[m],
+                {"section": section},
+            )
+            for p in range(PARTS)
+        ]
 
     def expert_ffn(m, b):
         quads = (starts[b + 1] - starts[b]) // nx
@@ -307,7 +326,7 @@
             hidden[used, cols] = (gated / (1.0 + jnp.exp(-gated)) * upward).astype(BF16)
             return 0
 
-        lax.fori_loop(0, w_gate.shape[1] // piece, inner, 0)
+        lax.fori_loop(0, w_gate.shape[1] // piece, inner, 0, unroll=True)
         now = hidden[used]
 
         def outer(t, _):
@@ -321,7 +340,7 @@
                     ]
             return 0
 
-        lax.fori_loop(0, PARTS // 2, outer, 0)
+        lax.fori_loop(0, PARTS // 2, outer, 0, unroll=True)
         sending = produced.reshape(slots, part_width)
         for q in range(quads):
             sending[quad(starts[b] // nx + q)] = dot(regroup_t[...], paired[q]).astype(BF16)
@@ -340,9 +359,8 @@
         def _():
             for copy in side(m, s):
                 copy.wait_recv()
-            combine[...] = combining(naming_before[m, 0], naming_before[m, 1])
+            combining(naming_before[m, 0], naming_before[m, 1])
             states[m] = (states_before[m].astype(F32) + mixed_rows(combine, m)).astype(BF16)
-            give(m, s - 1).start()
 
         @pl.when(jnp.logical_and(s == 0, m > 0))
         def _():
@@ -386,9 +404,14 @@
             for copy in side(m, s + 1):
                 copy.start()
 
+        @pl.when(s > 0)
+        def _():
+            for copy in give(m, s - 1):
+                copy.start()
+
         @pl.when(jnp.logical_and(m == 0, s == 0))
         def _():
-            lax.fori_loop(1, micro, prepare, 0)
+            prepare_rest()
 
         @pl.when(m == 0)
         def _():
@@ -444,8 +467,10 @@
 
         @pl.when(last)
         def _():
-            combine[...] = combining(naming[m, 0], naming[m, 1])
-            out[m] = (states[m].astype(F32) + mixed_rows(combine, micro + m)).astype(BF16)
+            combining(naming[m, 0], naming[m, 1])
+            result = (states[m].astype(F32) + mixed_rows(combine, micro + m)).astype(BF16)
+            for p in range(PARTS):
+                out[m, :, p * part_width : (p + 1) * part_width] = result[p * rows : (p + 1) * rows]
 
         for b in range(len(batches)):
             wait_sent(produced, b, r_send)
@@ -475,12 +500,12 @@
         for m in range(micro):
             for copy in side(m, s + 1):
                 copy.wait_send()
-            give(m, s).wait_recv()
+            remote(out.at[m], out.at[m], o_send.at[m], o_recv.at[m], {"section": s}).wait_recv()
 
     @pl.when(s > 0)
     def _():
         for m in range(micro):
-            give(m, s - 1).wait_send()
+            remote(states.at[m], states.at[m], o_send.at[m], o_recv.at[m], {"section": s}).wait_send()
 
 
 def on_device(sizes, tokens, norm_gain, router_weight, gate_weight, up_weight, down_weight, routing):
@@ -500,7 +525,7 @@
     outputs, gradient = pl.pallas_call(
         functools.partial(kernel, sizes),
         out_shape=(
-            jax.ShapeDtypeStruct((micro, stacked, part), BF16),
+            jax.ShapeDtypeStruct((micro, rows, width), BF16),
             jax.ShapeDtypeStruct((experts, width // replicas), F32),
         ),
         in_specs=[hbm] * 7,
@@ -518,8 +543,8 @@
             pltpu.VMEM((micro, rows, experts), F32),
             pltpu.VMEM((micro, rows, experts), F32),
             pltpu.VMEM((micro, slots, stacked), BF16),
-            pltpu.VMEM((slots, stacked), F32),
-            pltpu.VMEM((stacked, slots), F32),
+            pltpu.VMEM((GROUP, stacked), F32),
+            pltpu.VMEM((PARTS, slots), F32),
             pltpu.VMEM((slots, experts), BF16),
             pltpu.VMEM((slots // 8, 8, part), BF16),
             pltpu.VMEM((micro, slots // 8, 8, part), BF16),
@@ -559,7 +584,6 @@
             collective_id=0, has_side_effects=True, vmem_limit_bytes=58 * 1024 * 1024
         ),
     )(tokens, norm_gain, router_weight[0].T, routing[0].transpose(2, 0, 1), gate_weight[0, 0], up_weight[0, 0], down_weight[0, 0])
-    outputs = outputs.reshape(micro, PARTS, rows, part).transpose(0, 2, 1, 3).reshape(micro, rows, width)
     return outputs[None], gradient.T[None]
 
 

time: 381 us -> 364 us (0.955)
  Pallas kernels: 376 us -> 360 us
    pallas_call x1, Pallas kernels: 376 us -> 360 us  [on_device(): pl.pallas_call(functools.partial(kernel, sizes), out_shape=(jax.ShapeDtyp...]
where the time goes in v3:
time: 364 us; the launch traced here: 363 us
  Pallas kernels  360 us (99%)
    pallas_call x1, Pallas kernels, on_device(): pl.pallas_call(functools.partial(kernel, sizes), out_shape=(jax.ShapeDtyp...  360 us

profile of v3, /device:TPU:25, one launch (start us, length us, event | category | flops | bytes accessed | tf_op | source)
XLA Modules:
  0.0 363.4 jit_solution(1915392034942867549)
XLA Ops:
  0.6 359.6 %shard_map.86 = (bf16[4,32,2048]{2,1,0:T(8,128)(2,1)}, f32[32,64]{1,0:T(8,128)}) custom-call(bf16[4,32,2048]{2,1,0:T(8,128)(2,1)} %tokens_hbm.1, bf16[1,2048]{1,0:T(2,128)(2,1)} %gain_hbm.1, bf16[32,2048]{1,0:T(8,128)(2,1)} %bitcast.17, s32[6,4,32]{2,1,0:T(4,128)} %bitcast.19, bf16[2048,768]{1,0:T(8,128)(2,1)} %bitcast.13, bf16[2048,768]{1,0:T(8,128)(2,1)} %bitcast.14, ...), custom_call_target="tpu_custom_call" | custom-call | tf_op jit(solution)/shard_map/pallas_call | solution.py:525
  360.2 1.9 copy.11
  362.1 1.3 copy.12

commit v4 on v3

--- a/solution.py
+++ b/solution.py
@@ -101,6 +101,7 @@
     g_send,
     g_recv,
     go,
+    quiet,
 ):
     sections, nx, nz, total_rows = sizes
     micro, rows, width = out.shape
@@ -354,6 +355,27 @@
             total = part if total is None else total + part
         return total
 
+    def gradient_out():
+        part = count_in.at[pl.ds(0, replicas - 1)]
+        remote(part, part, c_send, c_recv, ahead(0)).wait()
+        total = jnp.sum(count_in[...], axis=0)[0:1]
+        share = experts * total / (topk * total_rows)
+        for mm in range(micro):
+            p = slope_all[mm]
+            slope_all[mm] = p * (share - jnp.sum(p * share, axis=-1, keepdims=True))
+        slope = slope_all[...].reshape(micro * rows, experts)
+        high = slope.astype(BF16)
+        low = (slope - high.astype(F32)).astype(BF16)
+        for t in range(width // 128):
+            h, c = divmod(t * 128, part_width)
+            some = normed_all[:, h * rows : (h + 1) * rows, c : c + 128].reshape(micro * rows, 128)
+            grad_own[t] = (dot_tn(high, some) + dot_tn(low, some)).astype(BF16)
+        for j in others:
+            k, i = order[j]
+            where = lax.rem(x + i, nx) * nz + lax.rem(z + k, nz)
+            remote(grad_own.at[where // 2], grad_in.at[j], g_send, g_recv, ahead(j)).start()
+        grad_in[own] = grad_own[(x * nz + z) // 2]
+
     def one(m, _):
         @pl.when(s > 0)
         def _():
@@ -443,27 +465,9 @@
                             produced.at[at(j)], returned.at[micro + m, at(j)], r_recv.at[micro + m, b]
                         ).start()
 
-        @pl.when(m == micro - 1)
-        def _():
-            part = count_in.at[pl.ds(0, replicas - 1)]
-            remote(part, part, c_send, c_recv, ahead(0)).wait()
-            total = jnp.sum(count_in[...], axis=0)[0:1]
-            share = experts * total / (topk * total_rows)
-            for mm in range(micro):
-                p = slope_all[mm]
-                slope_all[mm] = p * (share - jnp.sum(p * share, axis=-1, keepdims=True))
-            slope = slope_all[...].reshape(micro * rows, experts)
-            high = slope.astype(BF16)
-            low = (slope - high.astype(F32)).astype(BF16)
-            for t in range(width // 128):
-                h, c = divmod(t * 128, part_width)
-                some = normed_all[:, h * rows : (h + 1) * rows, c : c + 128].reshape(micro * rows, 128)
-                grad_own[t] = (dot_tn(high, some) + dot_tn(low, some)).astype(BF16)
-            for j in others:
-                k, i = order[j]
-                where = lax.rem(x + i, nx) * nz + lax.rem(z + k, nz)
-                remote(grad_own.at[where // 2], grad_in.at[j], g_send, g_recv, ahead(j)).start()
-            grad_in[own] = grad_own[(x * nz + z) // 2]
+        @pl.when(jnp.logical_and(m == micro - 1, s >= sections - 2))
+        def _():
+            gradient_out()
 
         @pl.when(last)
         def _():
@@ -483,9 +487,33 @@
         def _():
             pl.semaphore_signal(go, inc=1, device_id={"section": 0}, device_id_type=MESH)
 
+        @pl.when(jnp.logical_and(m == micro - 1, jnp.logical_and(s < sections - 2, lax.rem(s, 2) == 1)))
+        def _():
+            pl.semaphore_signal(quiet, inc=1, device_id={"section": s - 1}, device_id_type=MESH)
+
         return 0
 
     lax.fori_loop(0, micro, one, 0)
+
+    @pl.when(jnp.logical_not(last))
+    def _():
+        for m in range(micro):
+            for copy in side(m, s + 1):
+                copy.wait_send()
+            remote(out.at[m], out.at[m], o_send.at[m], o_recv.at[m], {"section": s}).wait_recv()
+
+    @pl.when(s > 0)
+    def _():
+        for m in range(micro):
+            remote(states.at[m], states.at[m], o_send.at[m], o_recv.at[m], {"section": s}).wait_send()
+
+    @pl.when(jnp.logical_and(s < sections - 2, lax.rem(s, 2) == 0))
+    def _():
+        pl.semaphore_wait(quiet, 1)
+
+    @pl.when(s < sections - 2)
+    def _():
+        gradient_out()
 
     part = grad_in.at[pl.ds(0, replicas - 1)]
     remote(part, part, g_send, g_recv, ahead(0)).wait()
@@ -494,18 +522,6 @@
     grad[...] = jnp.where(lax.rem(z, 2) == 0, summed[:, :take], summed[:, take:])
     for b in range(len(batches)):
         wait_sent(sent, b, d_send)
-
-    @pl.when(jnp.logical_not(last))
-    def _():
-        for m in range(micro):
-            for copy in side(m, s + 1):
-                copy.wait_send()
-            remote(out.at[m], out.at[m], o_send.at[m], o_recv.at[m], {"section": s}).wait_recv()
-
-    @pl.when(s > 0)
-    def _():
-        for m in range(micro):
-            remote(states.at[m], states.at[m], o_send.at[m], o_recv.at[m], {"section": s}).wait_send()
 
 
 def on_device(sizes, tokens, norm_gain, router_weight, gate_weight, up_weight, down_weight, routing):
@@ -579,6 +595,7 @@
             dma(()),
             dma(()),
             pltpu.SemaphoreType.REGULAR,
+            pltpu.SemaphoreType.REGULAR,
         ],
         compiler_params=pltpu.CompilerParams(
             collective_id=0, has_side_effects=True, vmem_limit_bytes=58 * 1024 * 1024

time: 364 us -> 363 us (level)
  no operation moved by 1% of the time
where the time goes in v4:
time: 363 us
  Pallas kernels  359 us (99%)
    pallas_call x1, Pallas kernels, on_device(): pl.pallas_call(functools.partial(kernel, sizes), out_shape=(jax.ShapeDtyp...  359 us

profile of v4, /device:TPU:25, one launch (start us, length us, event | category | flops | bytes accessed | tf_op | source)
XLA Modules:
  0.0 362.6 jit_solution(15185127432956015465)
XLA Ops:
  0.6 358.8 %shard_map.86 = (bf16[4,32,2048]{2,1,0:T(8,128)(2,1)}, f32[32,64]{1,0:T(8,128)}) custom-call(bf16[4,32,2048]{2,1,0:T(8,128)(2,1)} %tokens_hbm.1, bf16[1,2048]{1,0:T(2,128)(2,1)} %gain_hbm.1, bf16[32,2048]{1,0:T(8,128)(2,1)} %bitcast.17, s32[6,4,32]{2,1,0:T(4,128)} %bitcast.19, bf16[2048,768]{1,0:T(8,128)(2,1)} %bitcast.13, bf16[2048,768]{1,0:T(8,128)(2,1)} %bitcast.14, ...), custom_call_target="tpu_custom_call" | custom-call | tf_op jit(solution)/shard_map/pallas_call | solution.py:541
  359.4 1.9 copy.11
  361.3 1.3 copy.12
